TPU v7x, 128 devices: a whole 4x4x4 slice. The times are simulated.
128 devices in a mesh: energy: 32 (over y, z_lo, x), blk: 4 (over z_hi, core).
Axes of the slice: x: 4, y: 4, z: 4 (z_hi: 2, z_lo: 2; z = z_hi * 2 + z_lo), core: 2. Of those that a mesh axis runs over, the one named last changes fastest.
Arguments:
- lesser_green: bfloat16 [64, 4, 2, 384, 384], P('energy', 'blk'), may hold values from -4.1875 to 4.1875
- greater_green: bfloat16 [64, 4, 2, 384, 384], P('energy', 'blk'), may hold values from -4.1875 to 4.1875
- coulomb_blocks: bfloat16 [4, 3, 2, 384, 384], P('blk'), may hold values from -0.21875 to 0.21875
Outputs:
- lesser_sigma: bfloat16 [64, 4, 2, 384, 384], P('energy', 'blk')
- greater_sigma: bfloat16 [64, 4, 2, 384, 384], P('energy', 'blk')
All inputs are finite; a program needn't handle non-finite values.
Results may differ from a plain program's by a relative error of at most 0.017.
Values may be sent and summed in bfloat16 or wider, within the bound.
A program may use at most 128 MiB of HBM per device.

v0:
```python
import math

import jax
import jax.numpy as jnp
from jax import lax
from jax.sharding import PartitionSpec as P

good_precision = lax.Precision.HIGH


def for_sending(array):
    return jax.tree.map(lambda a: a.astype(jnp.bfloat16) if a.dtype == jnp.float32 else a, array)


def extended(block, sides, width):
    for axis, dim in sides:
        count = lax.axis_size(axis)
        forward = [(i, i + 1) for i in range(count - 1)]
        backward = [(target, source) for source, target in forward]
        low = lax.ppermute(
            lax.slice_in_dim(block, block.shape[dim] - width, None, axis=dim), axis, forward
        )
        high = lax.ppermute(lax.slice_in_dim(block, 0, width, axis=dim), axis, backward)
        block = jnp.concatenate([low, block, high], axis=dim)
    return block


def tables(pieces, inner):
    total = pieces * inner
    length = 2 * total
    frequency = lax.iota(jnp.int32, length)
    energies = lax.iota(jnp.int32, total)
    phase_index = frequency[:, None] * energies[None, :] % length
    angles = 2.0 * math.pi / length * phase_index.astype(jnp.float32)
    cosine_table = jnp.cos(angles).reshape(length, pieces, inner)
    sine_table = jnp.sin(angles).reshape(length, pieces, inner)
    return (cosine_table, sine_table)


def split_table(table):
    high_part = table.astype(jnp.bfloat16)
    low_part = (table - high_part.astype(jnp.float32)).astype(jnp.bfloat16)
    return (high_part, low_part)


def split_parts(values):
    return (values[:, :, :, 0], values[:, :, :, 1])


def join_parts(values):
    return jnp.stack([values[0], values[1]], axis=3).astype(jnp.bfloat16)


def apply_split(table_pair, data):
    form = "lek,egkrm->lgrm"
    return jnp.einsum(form, table_pair[0], data, preferred_element_type=jnp.float32) + jnp.einsum(
        form, table_pair[1], data, preferred_element_type=jnp.float32
    )


def forward(values, cosine_split, sine_split):
    real_part, imag_part = values
    spec_re = apply_split(cosine_split, real_part) + apply_split(sine_split, imag_part)
    spec_im = apply_split(cosine_split, imag_part) - apply_split(sine_split, real_part)
    return (spec_re, spec_im)


def inverse(spectrum, cosine_table, sine_table, factor):
    spec_re, spec_im = spectrum
    form = "lek,lgrm->egkrm"
    out_re = jnp.einsum(form, cosine_table, spec_re, precision=good_precision) - jnp.einsum(
        form, sine_table, spec_im, precision=good_precision
    )
    out_im = jnp.einsum(form, cosine_table, spec_im, precision=good_precision) + jnp.einsum(
        form, sine_table, spec_re, precision=good_precision
    )
    return (factor * out_re, factor * out_im)


def to_elements(pair):
    pieces = lax.axis_size("energy")
    regrouped = (
        lax.all_to_all(pair[0], "energy", split_axis=3, concat_axis=0, tiled=True),
        lax.all_to_all(pair[1], "energy", split_axis=3, concat_axis=0, tiled=True),
    )
    groups = 1
    return tuple(
        (
            member.reshape(pieces, groups, -1, 2, member.shape[3], member.shape[4])
            for member in regrouped
        )
    )


def to_energies(pair):
    flat = tuple((member.reshape(-1, 1, 2, member.shape[4], member.shape[5]) for member in pair))
    return jax.tree.map(
        lambda part, own: part.astype(own.dtype),
        lax.all_to_all(for_sending(flat), "energy", split_axis=0, concat_axis=3, tiled=True),
        flat,
    )


def congruence(coupling, padded):
    form_left = "ij,qejk->qeik"
    form_right = "qeik,jk->qeij"
    total_re = None
    total_im = None
    for offset in range(3):
        coul_re = coupling[offset, 0]
        coul_im = coupling[offset, 1]
        pol_re = padded[:, :, offset, 0]
        pol_im = padded[:, :, offset, 1]
        left_re = (
            jnp.einsum(form_left, coul_re, pol_re, preferred_element_type=jnp.float32)
            - jnp.einsum(form_left, coul_im, pol_im, preferred_element_type=jnp.float32)
        ).astype(jnp.bfloat16)
        left_im = (
            jnp.einsum(form_left, coul_re, pol_im, preferred_element_type=jnp.float32)
            + jnp.einsum(form_left, coul_im, pol_re, preferred_element_type=jnp.float32)
        ).astype(jnp.bfloat16)
        right_re = jnp.einsum(
            form_right, left_re, coul_re, preferred_element_type=jnp.float32
        ) + jnp.einsum(form_right, left_im, coul_im, preferred_element_type=jnp.float32)
        right_im = jnp.einsum(
            form_right, left_im, coul_re, preferred_element_type=jnp.float32
        ) - jnp.einsum(form_right, left_re, coul_im, preferred_element_type=jnp.float32)
        if total_re is None:
            total_re, total_im = (right_re, right_im)
        else:
            total_re = total_re + right_re
            total_im = total_im + right_im
    return jnp.stack([total_re, total_im], axis=2).astype(jnp.bfloat16)


def local(lesser_green, greater_green, coulomb_blocks):
    pieces = lax.axis_size("energy")
    inner = lesser_green.shape[0]
    total = pieces * inner
    length = 2 * total
    cosine_table, sine_table = tables(pieces, inner)
    cosine_split = split_table(cosine_table)
    sine_split = split_table(sine_table)
    less_elem, great_elem = to_elements((lesser_green, greater_green))
    less_spec = forward(split_parts(less_elem), cosine_split, sine_split)
    great_spec = forward(split_parts(great_elem), cosine_split, sine_split)
    cross_re = less_spec[0] * great_spec[0] + less_spec[1] * great_spec[1]
    cross_im = less_spec[1] * great_spec[0] - less_spec[0] * great_spec[1]
    pol_factor = -1.0 / (math.sqrt(total) * length)
    pol_less = join_parts(inverse((cross_re, cross_im), cosine_table, sine_table, pol_factor))
    pol_great = join_parts(inverse((cross_re, -cross_im), cosine_table, sine_table, pol_factor))
    pol_less, pol_great = to_energies((pol_less, pol_great))
    stacked = jnp.stack([pol_less, pol_great])
    padded = extended(stacked, (("blk", 2),), 1)
    screened = congruence(coulomb_blocks[0], padded)
    screen_less, screen_great = to_elements((screened[0][:, None], screened[1][:, None]))
    wspec_less = forward(split_parts(screen_less), cosine_split, sine_split)
    wspec_great = forward(split_parts(screen_great), cosine_split, sine_split)
    sigma_factor = 1.0 / (math.sqrt(total) * length)
    mult_less = (
        less_spec[0] * wspec_less[0] - less_spec[1] * wspec_less[1],
        less_spec[0] * wspec_less[1] + less_spec[1] * wspec_less[0],
    )
    mult_great = (
        great_spec[0] * wspec_great[0] - great_spec[1] * wspec_great[1],
        great_spec[0] * wspec_great[1] + great_spec[1] * wspec_great[0],
    )
    sigma_less = join_parts(inverse(mult_less, cosine_table, sine_table, sigma_factor))
    sigma_great = join_parts(inverse(mult_great, cosine_table, sine_table, sigma_factor))
    lesser_sigma, greater_sigma = to_energies((sigma_less, sigma_great))
    return (lesser_sigma, greater_sigma)


def solution(mesh):
    return jax.shard_map(
        local,
        mesh=mesh,
        in_specs=(
            P("energy", "blk", None, None, None),
            P("energy", "blk", None, None, None),
            P("blk", None, None, None, None),
        ),
        out_specs=(P("energy", "blk", None, None, None), P("energy", "blk", None, None, None)),
        check_vma=False,
    )
```

profile of v0, /device:TPU:1, one launch (start us, length us, event | category | flops | bytes accessed | tf_op | source)
XLA Modules:
  0.0 292.7 jit_solution(17960332847968507411)
XLA Ops:
  0.6 3.6 %copy.107 = bf16[2,1,2,384,384]{4,2,1,0,3:T(2,128)(2,1)} copy(bf16[2,1,2,384,384]{4,3,2,1,0:T(8,128)(2,1)} %param.3) | data formatting | bytes 2359296 | tf_op args[0]
  4.2 9.2 %all-to-all-start = ((bf16[2,1,2,384,384]{4,2,1,0,3:T(2,128)(2,1)}), bf16[2,1,2,384,384]{4,2,1,0,3:T(2,128)(2,1)S(1)}, u32[]{:S(2)}, u32[]{:S(2)}) async-start(bf16[2,1,2,384,384]{4,2,1,0,3:T(2,128)(2,1)} %copy.107), calls=%async_computation | async-start | bytes 2359296 | tf_op jit(solution)/shard_map/all_to_all | solution.py:83
  15.7 14.6 %all-to-all-done = bf16[2,1,2,384,384]{4,2,1,0,3:T(2,128)(2,1)S(1)} async-done(((bf16[2,1,2,384,384]{4,2,1,0,3:T(2,128)(2,1)}), bf16[2,1,2,384,384]{4,2,1,0,3:T(2,128)(2,1)S(1)}, u32[]{:S(2)}, u32[]{:S(2)}) %all-to-all-start) | async-done | bytes 1179680 | tf_op jit(solution)/shard_map/all_to_all | solution.py:83
  30.3 4.8 %all-to-all-start.1 = ((bf16[2,1,2,384,384]{4,2,1,0,3:T(2,128)(2,1)}), bf16[2,1,2,384,384]{4,2,1,0,3:T(2,128)(2,1)}, u32[]{:S(2)}, u32[]{:S(2)}) async-start(bf16[2,1,2,384,384]{4,2,1,0,3:T(2,128)(2,1)} %copy.110), calls=%async_computation.1 | async-start | bytes 2359296 | tf_op jit(solution)/shard_map/all_to_all | solution.py:84
  40.4 10.0 %all-to-all-done.1 = bf16[2,1,2,384,384]{4,2,1,0,3:T(2,128)(2,1)} async-done(((bf16[2,1,2,384,384]{4,2,1,0,3:T(2,128)(2,1)}), bf16[2,1,2,384,384]{4,2,1,0,3:T(2,128)(2,1)}, u32[]{:S(2)}, u32[]{:S(2)}) %all-to-all-start.1) | async-done | bytes 1179680 | tf_op jit(solution)/shard_map/all_to_all | solution.py:84
  62.4 2.9 multiply_subtract_fusion.2
  69.6 3.0 %stack.62 = bf16[64,1,1,12,384]{4,0,3,2,1:T(8,128)(2,1)} reshape(bf16[32,1,2,12,384]{4,2,0,3,1:T(2,128)(2,1)} %copy.118) | data formatting | bytes 1179648 | tf_op jit(solution)/shard_map/stack | solution.py:51
  75.0 2.7 stack.61
  81.2 5.6 %all-to-all-start.3 = ((bf16[64,1,2,12,384]{4,2,3,1,0:T(2,128)(2,1)}), bf16[64,1,2,12,384]{4,2,3,1,0:T(2,128)(2,1)}, u32[]{:S(2)}, u32[]{:S(2)}) async-start(bf16[64,1,2,12,384]{4,2,3,1,0:T(2,128)(2,1)} %copy.119), calls=%async_computation.3 | async-start | bytes 2359296 | tf_op jit(solution)/shard_map/all_to_all | solution.py:99
  97.4 4.5 %all-to-all-done.3 = bf16[64,1,2,12,384]{4,2,3,1,0:T(2,128)(2,1)} async-done(((bf16[64,1,2,12,384]{4,2,3,1,0:T(2,128)(2,1)}), bf16[64,1,2,12,384]{4,2,3,1,0:T(2,128)(2,1)}, u32[]{:S(2)}, u32[]{:S(2)}) %all-to-all-start.3) | async-done | bytes 1179680 | tf_op jit(solution)/shard_map/all_to_all | solution.py:99
  101.9 5.6 %all-to-all-start.2 = ((bf16[64,1,2,12,384]{4,2,3,1,0:T(2,128)(2,1)}), bf16[64,1,2,12,384]{4,2,3,1,0:T(2,128)(2,1)S(1)}, u32[]{:S(2)}, u32[]{:S(2)}) async-start(bf16[64,1,2,12,384]{4,2,3,1,0:T(2,128)(2,1)} %copy.115), calls=%async_computation.2 | async-start | bytes 2359296 | tf_op jit(solution)/shard_map/all_to_all | solution.py:99
  111.6 10.9 %all-to-all-done.2 = bf16[64,1,2,12,384]{4,2,3,1,0:T(2,128)(2,1)S(1)} async-done(((bf16[64,1,2,12,384]{4,2,3,1,0:T(2,128)(2,1)}), bf16[64,1,2,12,384]{4,2,3,1,0:T(2,128)(2,1)S(1)}, u32[]{:S(2)}, u32[]{:S(2)}) %all-to-all-start.2) | async-done | bytes 1179680 | tf_op jit(solution)/shard_map/all_to_all | solution.py:99
  125.6 6.3 %collective-permute-start.1 = (bf16[2,2,1,2,384,384]{4,5,1,0,3,2:T(8,128)(2,1)S(1)}, bf16[2,2,1,2,384,384]{4,5,1,0,3,2:T(8,128)(2,1)S(1)}, u32[]{:S(2)}, u32[]{:S(2)}) collective-permute-start(bf16[2,2,1,2,384,384]{4,5,1,0,3,2:T(8,128)(2,1)S(1)} %pad_maximum_fusion), channel_id=1, source_target_pairs={{1,0},{2,1},{3,2},{5,4},{6,5},{7,6},{9,8},{10,9},{11,10},{13,12},{... | collective-permute-start | bytes 7077896 | tf_op jit(solution)/shard_map/ppermute | solution.py:23
  131.9 5.3 %collective-permute-start = (bf16[2,2,1,2,384,384]{4,5,1,0,3,2:T(8,128)(2,1)S(1)}, bf16[2,2,1,2,384,384]{4,5,1,0,3,2:T(8,128)(2,1)S(1)}, u32[]{:S(2)}, u32[]{:S(2)}) collective-permute-start(bf16[2,2,1,2,384,384]{4,5,1,0,3,2:T(8,128)(2,1)S(1)} %pad_maximum_fusion), channel_id=1, source_target_pairs={{0,1},{1,2},{2,3},{4,5},{5,6},{6,7},{8,9},{9,10},{10,11},{12,13},{... | collective-permute-start | bytes 7077896 | tf_op jit(solution)/shard_map/ppermute | solution.py:20
  144.6 18.1 %collective-permute-done = bf16[2,2,1,2,384,384]{4,5,1,0,3,2:T(8,128)(2,1)S(1)} collective-permute-done((bf16[2,2,1,2,384,384]{4,5,1,0,3,2:T(8,128)(2,1)S(1)}, bf16[2,2,1,2,384,384]{4,5,1,0,3,2:T(8,128)(2,1)S(1)}, u32[]{:S(2)}, u32[]{:S(2)}) %collective-permute-start) | collective-permute-done | bytes 2359328 | tf_op jit(solution)/shard_map/ppermute | solution.py:20
  181.0 4.3 %all-to-all-start.4 = ((bf16[2,1,2,384,384]{4,0,2,1,3:T(2,128)(2,1)}), bf16[2,1,2,384,384]{4,0,2,1,3:T(2,128)(2,1)S(1)}, u32[]{:S(2)}, u32[]{:S(2)}) async-start(bf16[2,1,2,384,384]{4,0,2,1,3:T(2,128)(2,1)} %copy.135), calls=%async_computation.4 | async-start | bytes 2359296 | tf_op jit(solution)/shard_map/all_to_all | solution.py:83
  187.5 14.1 %all-to-all-done.4 = bf16[2,1,2,384,384]{4,0,2,1,3:T(2,128)(2,1)S(1)} async-done(((bf16[2,1,2,384,384]{4,0,2,1,3:T(2,128)(2,1)}), bf16[2,1,2,384,384]{4,0,2,1,3:T(2,128)(2,1)S(1)}, u32[]{:S(2)}, u32[]{:S(2)}) %all-to-all-start.4) | async-done | bytes 1179680 | tf_op jit(solution)/shard_map/all_to_all | solution.py:83
  201.7 4.7 %all-to-all-start.6 = ((bf16[2,1,2,384,384]{4,0,2,1,3:T(2,128)(2,1)}), bf16[2,1,2,384,384]{4,0,2,1,3:T(2,128)(2,1)S(1)}, u32[]{:S(2)}, u32[]{:S(2)}) async-start(bf16[2,1,2,384,384]{4,0,2,1,3:T(2,128)(2,1)} %copy.142), calls=%async_computation.6 | async-start | bytes 2359296 | tf_op jit(solution)/shard_map/all_to_all | solution.py:84
  236.1 2.8 stack.70
  244.6 7.7 %all-to-all-start.5 = ((bf16[64,1,2,12,384]{4,2,3,1,0:T(2,128)(2,1)}), bf16[64,1,2,12,384]{4,2,3,1,0:T(2,128)(2,1)}, u32[]{:S(2)}, u32[]{:S(2)}) async-start(bf16[64,1,2,12,384]{4,2,3,1,0:T(2,128)(2,1)} %copy.140), calls=%async_computation.5 | async-start | bytes 2359296 | tf_op jit(solution)/shard_map/all_to_all | solution.py:99
  252.4 3.2 %fusion.8 = f32[128,12,384]{2,0,1:T(8,128)S(1)} fusion(f32[128,12,384,1]{2,0,3,1:T(8,128)S(1)} %copy-done.12, f32[128,12,384,1]{2,0,3,1:T(8,128)} %fusion.174, f32[128,12,384,1]{2,0,3,1:T(8,128)} %fusion.175, bf16[32,1,2,2,12,384]{5,0,2,4,3,1:T(8,128)(2,1)S(1)} %bitcast.600, s32[32,2]{0,1:T(2,128)S(1)} %multiply_add_fusion.3), kind=kOutput, calls=%fused_computation.16 | convolution fusion | flops 77414400 | bytes 10028032 | tf_op jit(solution)/shard_map/lek,egkrm->lgrm/dot_general | solution.py:56
  257.5 3.2 %multiply_add_fusion = (f32[128,12,384]{2,0,1:T(8,128)S(1)}, f32[128,12,384]{2,0,1:T(8,128)S(1)}) fusion(f32[128,12,384]{2,0,1:T(8,128)S(1)} %copy-done.3, f32[128,12,384]{2,0,1:T(8,128)S(1)} %copy-done.5, f32[128,12,384]{2,0,1:T(8,128)S(1)} %fusion.8, bf16[32,1,2,2,12,384]{5,0,2,4,3,1:T(8,128)(2,1)S(1)} %bitcast.601, s32[32,2]{0,1:T(2,128)S(1)} %multiply_add_fusion.3, ...), kind=kOutput, calls=%fused_computation.59 | convolution fusion | flops 80953344 | bytes 19465216 | tf_op jit(solution)/shard_map/lek,egkrm->lgrm/dot_general | solution.py:56
  270.6 7.7 %all-to-all-start.7 = ((bf16[64,1,2,12,384]{4,2,3,1,0:T(2,128)(2,1)}), bf16[64,1,2,12,384]{4,2,3,1,0:T(2,128)(2,1)S(1)}, u32[]{:S(2)}, u32[]{:S(2)}) async-start(bf16[64,1,2,12,384]{4,2,3,1,0:T(2,128)(2,1)} %copy.147), calls=%async_computation.7 | async-start | bytes 2359296 | tf_op jit(solution)/shard_map/all_to_all | solution.py:99
  281.5 8.9 %all-to-all-done.7 = bf16[64,1,2,12,384]{4,2,3,1,0:T(2,128)(2,1)S(1)} async-done(((bf16[64,1,2,12,384]{4,2,3,1,0:T(2,128)(2,1)}), bf16[64,1,2,12,384]{4,2,3,1,0:T(2,128)(2,1)S(1)}, u32[]{:S(2)}, u32[]{:S(2)}) %all-to-all-start.7) | async-done | bytes 1179680 | tf_op jit(solution)/shard_map/all_to_all | solution.py:99
  (149 shorter events, 127.0 us)
Async XLA Ops:
  0.6 12.8 %copy-start.19 = (bf16[2,1,2,384,384]{4,3,2,1,0:T(8,128)(2,1)S(1)}, bf16[2,1,2,384,384]{4,3,2,1,0:T(8,128)(2,1)}, u32[]{:S(2)}) copy-start(bf16[2,1,2,384,384]{4,3,2,1,0:T(8,128)(2,1)} %param.4) | copy-start | bytes 3538948
  4.2 26.1 %all-to-all-start = ((bf16[2,1,2,384,384]{4,2,1,0,3:T(2,128)(2,1)}), bf16[2,1,2,384,384]{4,2,1,0,3:T(2,128)(2,1)S(1)}, u32[]{:S(2)}, u32[]{:S(2)}) async-start(bf16[2,1,2,384,384]{4,2,1,0,3:T(2,128)(2,1)} %copy.107), calls=%async_computation | async-start | bytes 2359296 | tf_op jit(solution)/shard_map/all_to_all | solution.py:83
  30.3 20.1 %all-to-all-start.1 = ((bf16[2,1,2,384,384]{4,2,1,0,3:T(2,128)(2,1)}), bf16[2,1,2,384,384]{4,2,1,0,3:T(2,128)(2,1)}, u32[]{:S(2)}, u32[]{:S(2)}) async-start(bf16[2,1,2,384,384]{4,2,1,0,3:T(2,128)(2,1)} %copy.110), calls=%async_computation.1 | async-start | bytes 2359296 | tf_op jit(solution)/shard_map/all_to_all | solution.py:84
  56.8 1.7 copy-start.14
  57.5 1.9 copy-start.13
  60.3 1.5 copy-start.6
  62.4 2.9 copy-start.4
  81.2 20.7 %all-to-all-start.3 = ((bf16[64,1,2,12,384]{4,2,3,1,0:T(2,128)(2,1)}), bf16[64,1,2,12,384]{4,2,3,1,0:T(2,128)(2,1)}, u32[]{:S(2)}, u32[]{:S(2)}) async-start(bf16[64,1,2,12,384]{4,2,3,1,0:T(2,128)(2,1)} %copy.119), calls=%async_computation.3 | async-start | bytes 2359296 | tf_op jit(solution)/shard_map/all_to_all | solution.py:99
  101.9 20.6 %all-to-all-start.2 = ((bf16[64,1,2,12,384]{4,2,3,1,0:T(2,128)(2,1)}), bf16[64,1,2,12,384]{4,2,3,1,0:T(2,128)(2,1)S(1)}, u32[]{:S(2)}, u32[]{:S(2)}) async-start(bf16[64,1,2,12,384]{4,2,3,1,0:T(2,128)(2,1)} %copy.115), calls=%async_computation.2 | async-start | bytes 2359296 | tf_op jit(solution)/shard_map/all_to_all | solution.py:99
  125.3 11.9 %copy-start = (bf16[1,3,2,384,384]{4,3,2,1,0:T(8,128)(2,1)S(1)}, bf16[1,3,2,384,384]{4,3,2,1,0:T(8,128)(2,1)}, u32[]{:S(2)}) copy-start(bf16[1,3,2,384,384]{4,3,2,1,0:T(8,128)(2,1)} %param.5) | copy-start | bytes 5308420
  125.6 45.1 %collective-permute-start.1 = (bf16[2,2,1,2,384,384]{4,5,1,0,3,2:T(8,128)(2,1)S(1)}, bf16[2,2,1,2,384,384]{4,5,1,0,3,2:T(8,128)(2,1)S(1)}, u32[]{:S(2)}, u32[]{:S(2)}) collective-permute-start(bf16[2,2,1,2,384,384]{4,5,1,0,3,2:T(8,128)(2,1)S(1)} %pad_maximum_fusion), channel_id=1, source_target_pairs={{1,0},{2,1},{3,2},{5,4},{6,5},{7,6},{9,8},{10,9},{11,10},{13,12},{... | collective-permute-start | bytes 7077896 | tf_op jit(solution)/shard_map/ppermute | solution.py:23
  131.9 30.9 %collective-permute-start = (bf16[2,2,1,2,384,384]{4,5,1,0,3,2:T(8,128)(2,1)S(1)}, bf16[2,2,1,2,384,384]{4,5,1,0,3,2:T(8,128)(2,1)S(1)}, u32[]{:S(2)}, u32[]{:S(2)}) collective-permute-start(bf16[2,2,1,2,384,384]{4,5,1,0,3,2:T(8,128)(2,1)S(1)} %pad_maximum_fusion), channel_id=1, source_target_pairs={{0,1},{1,2},{2,3},{4,5},{5,6},{6,7},{8,9},{9,10},{10,11},{12,13},{... | collective-permute-start | bytes 7077896 | tf_op jit(solution)/shard_map/ppermute | solution.py:20
  181.0 20.6 %all-to-all-start.4 = ((bf16[2,1,2,384,384]{4,0,2,1,3:T(2,128)(2,1)}), bf16[2,1,2,384,384]{4,0,2,1,3:T(2,128)(2,1)S(1)}, u32[]{:S(2)}, u32[]{:S(2)}) async-start(bf16[2,1,2,384,384]{4,0,2,1,3:T(2,128)(2,1)} %copy.135), calls=%async_computation.4 | async-start | bytes 2359296 | tf_op jit(solution)/shard_map/all_to_all | solution.py:83
  201.7 16.9 %all-to-all-start.6 = ((bf16[2,1,2,384,384]{4,0,2,1,3:T(2,128)(2,1)}), bf16[2,1,2,384,384]{4,0,2,1,3:T(2,128)(2,1)S(1)}, u32[]{:S(2)}, u32[]{:S(2)}) async-start(bf16[2,1,2,384,384]{4,0,2,1,3:T(2,128)(2,1)} %copy.142), calls=%async_computation.6 | async-start | bytes 2359296 | tf_op jit(solution)/shard_map/all_to_all | solution.py:84
  210.8 1.7 copy-start.7
  210.8 2.4 copy-start.11
  231.8 2.1 copy-start.16
  242.4 9.9 %copy-start.12 = (f32[128,12,384,1]{2,0,3,1:T(8,128)S(1)}, f32[128,12,384,1]{2,0,3,1:T(8,128)}, u32[]{:S(2)}) copy-start(f32[128,12,384,1]{2,0,3,1:T(8,128)} %fusion.171) | copy-start | bytes 7077892
  244.6 25.9 %all-to-all-start.5 = ((bf16[64,1,2,12,384]{4,2,3,1,0:T(2,128)(2,1)}), bf16[64,1,2,12,384]{4,2,3,1,0:T(2,128)(2,1)}, u32[]{:S(2)}, u32[]{:S(2)}) async-start(bf16[64,1,2,12,384]{4,2,3,1,0:T(2,128)(2,1)} %copy.140), calls=%async_computation.5 | async-start | bytes 2359296 | tf_op jit(solution)/shard_map/all_to_all | solution.py:99
  252.4 3.3 %copy-start.3 = (f32[128,12,384]{2,0,1:T(8,128)S(1)}, f32[128,12,384]{2,0,1:T(8,128)}, u32[]{:S(2)}) copy-start(f32[128,12,384]{2,0,1:T(8,128)} %copy-done.2) | copy-start | bytes 7077892
  252.4 3.8 %copy-start.5 = (f32[128,12,384]{2,0,1:T(8,128)S(1)}, f32[128,12,384]{2,0,1:T(8,128)}, u32[]{:S(2)}) copy-start(f32[128,12,384]{2,0,1:T(8,128)} %copy-done.4) | copy-start | bytes 7077892
  252.4 4.5 %copy-start.9 = (f32[128,12,384,1]{2,0,3,1:T(8,128)S(1)}, f32[128,12,384,1]{2,0,3,1:T(8,128)}, u32[]{:S(2)}) copy-start(f32[128,12,384,1]{2,0,3,1:T(8,128)} %fusion.176) | copy-start | bytes 7077892
  252.4 5.2 %copy-start.10 = (f32[128,12,384,1]{2,0,3,1:T(8,128)S(1)}, f32[128,12,384,1]{2,0,3,1:T(8,128)}, u32[]{:S(2)}) copy-start(f32[128,12,384,1]{2,0,3,1:T(8,128)} %fusion.172) | copy-start | bytes 7077892
  270.6 19.9 %all-to-all-start.7 = ((bf16[64,1,2,12,384]{4,2,3,1,0:T(2,128)(2,1)}), bf16[64,1,2,12,384]{4,2,3,1,0:T(2,128)(2,1)S(1)}, u32[]{:S(2)}, u32[]{:S(2)}) async-start(bf16[64,1,2,12,384]{4,2,3,1,0:T(2,128)(2,1)} %copy.147), calls=%async_computation.7 | async-start | bytes 2359296 | tf_op jit(solution)/shard_map/all_to_all | solution.py:99
  (6 other events, 7.1 us)
where the time goes:
time: 297 us; the launch traced here: 293 us
  matrix products  84.1 us (28%)
  waiting for transfers between devices  81.5 us (27%)
  local copies, waits for them, and re-layouts  61.9 us (21%)
  starting transfers between devices  61.2 us (21%)
    all_to_all x2, waiting for transfers between devices, to_elements(): lax.all_to_all(pair[0], 'energy', split_axis=3, concat_axis=0, tiled=True)  28.8 us
    all_to_all x4, starting transfers between devices, to_energies(): lax.all_to_all(for_sending(flat), 'energy', split_axis=0, concat_axis=3,...  26.6 us
    all_to_all x4, waiting for transfers between devices, to_energies(): lax.all_to_all(for_sending(flat), 'energy', split_axis=0, concat_axis=3,...  24.3 us
    dot_general x16, matrix products, apply_split(): jnp.einsum(form, table_pair[1], data, preferred_element_type=jnp.float32)  23.6 us
    another operation x12, local copies, waits for them, and re-layouts, join_parts(): return jnp.stack([values[0], values[1]], axis=3).astype(jnp.bfloat16)  21 us
    ppermute x1, waiting for transfers between devices, extended(): lax.ppermute(lax.slice_in_dim(block, block.shape[dim] - width, None, axis...  18.1 us
    dot_general x16, matrix products, apply_split(): jnp.einsum(form, table_pair[0], data, preferred_element_type=jnp.float32)  18.1 us
    unnamed x44, local copies, waits for them, and re-layouts  15.7 us
  transfers between devices with their start and end apart: 10, of which 8 were waited for; matrix products, arithmetic and copies ran while one was open for 23% of the time, Pallas kernels for 0%

commit v1 on v0

v1 whole, which is shorter than its diff:
```python
import functools
import math

import numpy as np
import jax
import jax.numpy as jnp
from jax import lax
from jax.experimental import pallas as pl
from jax.experimental.pallas import tpu as pltpu
from jax.sharding import PartitionSpec as P

MESH = pl.DeviceIdType.MESH
BF = jnp.bfloat16
F32 = jnp.float32
PIECES = 32
ROWS = 384
LANES = 128
NE = 64
LENGTH = 2 * NE


def dft_tables():
    f = np.arange(LENGTH)[:, None]
    e = np.arange(NE)[None, :]
    angle = 2.0 * math.pi / LENGTH * (f * e % LENGTH)
    cos, sin = np.cos(angle), np.sin(angle)
    fwd = np.zeros((2, 2, LENGTH, PIECES, 2, 2, 2))
    cs = cos.reshape(LENGTH, PIECES, 2)
    sn = sin.reshape(LENGTH, PIECES, 2)
    for k in range(2):
        fwd[k, 0, :, :, k, :, 0] = cs
        fwd[k, 0, :, :, k, :, 1] = sn
        fwd[k, 1, :, :, k, :, 0] = -sn
        fwd[k, 1, :, :, k, :, 1] = cs
    ct = cs.transpose(1, 2, 0)
    st = sn.transpose(1, 2, 0)
    scale = 1.0 / (math.sqrt(NE) * LENGTH)
    pol = np.zeros((PIECES, 2, 2, 2, 2, LENGTH))
    pol[:, 0, :, 0, 0] = ct
    pol[:, 0, :, 0, 1] = -st
    pol[:, 0, :, 1, 0] = st
    pol[:, 0, :, 1, 1] = ct
    pol[:, 1, :, 0, 0] = ct
    pol[:, 1, :, 0, 1] = st
    pol[:, 1, :, 1, 0] = st
    pol[:, 1, :, 1, 1] = -ct
    sig = np.zeros((PIECES, 2, 2, 2, 2, 2, LENGTH))
    for k in range(2):
        sig[:, k, :, 0, k, 0] = ct
        sig[:, k, :, 0, k, 1] = -st
        sig[:, k, :, 1, k, 0] = st
        sig[:, k, :, 1, k, 1] = ct
    as_bf = lambda a, m, n: jnp.asarray(a.reshape(m, n).astype(np.float32)).astype(BF)
    return (
        as_bf(fwd, 4 * LENGTH, 4 * NE),
        as_bf(-scale * pol, 4 * NE, 2 * LENGTH),
        as_bf(scale * sig, 4 * NE, 4 * LENGTH),
    )


def mirror(t):
    return (t // 8) * 8 + (1 - lax.rem(t // 4, 2)) * 4 + lax.rem(t, 4)


def dot(a, b):
    return jnp.dot(a, b, preferred_element_type=F32)


def kernel(
    lg, gg, cb, fwd_h, pol_h, sig_h, ol, og,
    gin, s0, xb, ps, pr, p3, lf, sc, ss, sx, fs, fr, ob, cc, rr, fwd, pol, sig,
    in_sem, tab_sem, self_sem, send_sem, recv_sem, near_send, near_recv, out_sem,
):
    me = lax.axis_index("energy")
    b = lax.axis_index("blk")
    upper = b >= 2
    my = me // 8
    mz = lax.rem(me // 4, 2)
    mx = lax.rem(me, 4)

    def lag_of(t):
        return jnp.where(upper, mirror(t), t)

    my_lag = lag_of(me)
    inner = jnp.logical_or(b == 1, b == 2)
    core_id = {"energy": me, "blk": b + 1 - 2 * lax.rem(b, 2)}
    cross_id = {"energy": mirror(me), "blk": 3 - b}

    def target(k):
        dz = lax.rem(k, 2)
        dx = lax.rem(k // 2, 4)
        dy = lax.rem(k // 8 + dx, 4)
        return lax.rem(my + dy, 4) * 8 + lax.rem(mz + dz, 2) * 4 + lax.rem(mx + dx, 4)

    def g_copy(c, a):
        src = (lg, gg)[a]
        return pltpu.make_async_copy(
            src.at[:, 0, :, :, pl.ds(LANES * c, LANES)], gin.at[c, a], in_sem.at[c, a]
        )

    for c in range(3):
        for a in range(2):
            g_copy(c, a).start()
    tables = [
        pltpu.make_async_copy(fwd_h, fwd, tab_sem.at[0]),
        pltpu.make_async_copy(pol_h, pol, tab_sem.at[1]),
        pltpu.make_async_copy(sig_h, sig, tab_sem.at[2]),
    ]
    for o in range(3):
        for r in range(2):
            tables.append(
                pltpu.make_async_copy(
                    cb.at[0, o, r], cc.at[o, :, pl.ds(ROWS * r, ROWS)], tab_sem.at[3 + 2 * o + r]
                )
            )
    for copy in tables:
        copy.start()

    barrier = pltpu.get_barrier_semaphore()

    def greet(k, carry):
        pl.semaphore_signal(
            barrier, inc=1, device_id={"energy": target(k), "blk": b}, device_id_type=MESH
        )
        return carry

    lax.fori_loop(1, PIECES, greet, 0)
    pl.semaphore_signal(barrier, inc=1, device_id=core_id, device_id_type=MESH)

    @pl.when(inner)
    def _():
        pl.semaphore_signal(barrier, inc=1, device_id=cross_id, device_id_type=MESH)

    def exchange(stage, part, source, dest, span):
        def go(k, carry):
            t = target(k)
            pltpu.make_async_remote_copy(
                src_ref=source(t), dst_ref=dest(), send_sem=send_sem.at[stage, part],
                recv_sem=recv_sem.at[stage, part], device_id={"energy": t, "blk": b},
                device_id_type=MESH,
            ).start()
            return carry

        lax.fori_loop(1, PIECES, go, 0)
        pltpu.make_async_copy(source(me), dest(), self_sem.at[stage, part]).start()

    def arrived(stage, part, source, dest, span):
        pltpu.make_async_copy(span, span, recv_sem.at[stage, part]).wait()
        pltpu.make_async_copy(source(me), dest(), self_sem.at[stage, part]).wait()

    def sent(stage, part, span):
        pltpu.make_async_copy(span, span, send_sem.at[stage, part]).wait()

    def st0(c):
        return (
            0, c, lambda t: s0.at[c, :, t], lambda: xb.at[c, :, :, me],
            xb.at[c, :, :, pl.ds(0, PIECES - 1)],
        )

    def st1(c):
        return (
            1, c, lambda t: ps.at[c, :, :, lag_of(t)], lambda: pr.at[c, :, me],
            pr.at[c, :, pl.ds(0, PIECES - 1)],
        )

    def st2(r):
        return (
            2, r, lambda t: ss.at[r, t], lambda: sx.at[r, :, :, my_lag],
            sx.at[r, :, :, pl.ds(0, PIECES - 1)],
        )

    def st3(r):
        return (
            3, r, lambda t: fs.at[r, :, :, t], lambda: fr.at[r, me],
            fr.at[r, pl.ds(0, PIECES - 1)],
        )

    for c in range(3):
        for a in range(2):
            g_copy(c, a).wait()

        def pack(i, carry):
            for r in range(3):
                x = gin[c, :, :, :, pl.ds(128 * r + 32 * i, 32), :].reshape(8, 32, LANES)
                s0[c, r, pl.ds(8 * i, 8)] = jnp.swapaxes(x, 0, 1).reshape(8, 4, 8, LANES)
            return carry

        lax.fori_loop(0, 4, pack, 0)
        if c == 0:
            pl.semaphore_wait(barrier, jnp.where(inner, PIECES + 1, PIECES))
        exchange(*st0(c))

    for copy in tables:
        copy.wait()
    for o in range(3):
        cre = cc[o, :, :ROWS].T
        cim = cc[o, :, ROWS:].T
        rr[o, :ROWS, :ROWS] = cre
        rr[o, ROWS:, ROWS:] = cre
        rr[o, ROWS:, :ROWS] = cim
        rr[o, :ROWS, ROWS:] = -cim

    @pl.when(b == 0)
    def _():
        lf[0] = jnp.zeros(lf.shape[1:], BF)

    @pl.when(b == 3)
    def _():
        lf[2] = jnp.zeros(lf.shape[1:], BF)

    def spectrum(x0, x1):
        x = jnp.concatenate([x0.reshape(256, LANES), x1.reshape(256, LANES)], axis=1)
        y = dot(fwd[...], x)
        n = LENGTH
        return y[:n], y[n : 2 * n], y[2 * n : 3 * n], y[3 * n :]

    for c in range(3):
        arrived(*st0(c))

        def correlate(i, carry):
            r, h = i // 2, 2 * lax.rem(i, 2)
            lre, lim, gre, gim = spectrum(xb[c, r, h], xb[c, r, h + 1])
            cross = jnp.concatenate(
                [lre * gre + lim * gim, lim * gre - lre * gim], axis=0
            ).astype(BF)
            p = dot(pol[...], cross).astype(BF)
            ps[c, r, h] = p[:, :LANES].reshape(PIECES, 8, LANES)
            ps[c, r, h + 1] = p[:, LANES:].reshape(PIECES, 8, LANES)
            return carry

        lax.fori_loop(0, 6, correlate, 0)
        exchange(*st1(c))

    def near(c, up):
        slot = 0 if up else 2
        return slot

    def near_copy(c, slot, device):
        return pltpu.make_async_remote_copy(
            src_ref=p3.at[1, c], dst_ref=p3.at[slot, c], send_sem=near_send.at[slot, c],
            recv_sem=near_recv.at[slot, c], device_id=device, device_id_type=MESH,
        )

    even = lax.rem(b, 2) == 0

    def left(o, c):
        def one(q, carry):
            pre = p3[o, c, 2 * q]
            pim = p3[o, c, 2 * q + 1]
            rhs = jnp.concatenate(
                [jnp.concatenate([pre, pim], axis=1), jnp.concatenate([-pim, pre], axis=1)], axis=0
            )
            v = dot(cc[o], rhs).astype(BF)
            for r in range(3):
                lf[o, r, q, :, LANES * c : LANES * c + LANES] = v[128 * r : 128 * r + 128, :LANES]
                lf[o, r, q, :, ROWS + LANES * c : ROWS + LANES * c + LANES] = v[
                    128 * r : 128 * r + 128, LANES:
                ]
            return carry

        lax.fori_loop(0, 4, one, 0)

    for c in range(3):
        arrived(*st1(c))

        def unpack(i, carry):
            for r in range(3):
                x = pr[c, r, pl.ds(8 * i, 8)].reshape(32, 8, LANES)
                p3[1, c, :, pl.ds(128 * r + 32 * i, 32), :] = jnp.swapaxes(x, 0, 1)
            return carry

        lax.fori_loop(0, 4, unpack, 0)

        @pl.when(b < 3)
        def _():
            dev = {"energy": jnp.where(even, me, mirror(me)), "blk": b + 1}
            near_copy(c, 0, dev).start()

        @pl.when(b > 0)
        def _():
            dev = {"energy": jnp.where(even, mirror(me), me), "blk": b - 1}
            near_copy(c, 2, dev).start()

        left(1, c)

    for c in range(3):
        @pl.when(b > 0)
        def _():
            near_copy(c, 0, core_id).wait_recv()
            left(0, c)

        @pl.when(b < 3)
        def _():
            near_copy(c, 2, core_id).wait_recv()
            left(2, c)

    def right(r, carry):
        for n in range(3):
            v = sum(
                dot(lf[o, r].reshape(512, 2 * ROWS), rr[o, :, 256 * n : 256 * n + 256])
                for o in range(3)
            ).astype(BF)
            for h in range(2):
                part, c = divmod(2 * n + h, 3)
                for q in range(4):
                    sc[c, 2 * q + part] = v[128 * q : 128 * q + 128, LANES * h : LANES * h + LANES]

        def pack(i, carry):
            for c in range(3):
                x = sc[c, :, pl.ds(32 * i, 32), :]
                ss[r, pl.ds(8 * i, 8), :, c] = jnp.swapaxes(x, 0, 1).reshape(8, 4, 8, LANES)
            return carry

        lax.fori_loop(0, 4, pack, 0)
        exchange(*st2(r))
        return carry

    lax.fori_loop(0, 3, right, 0)

    def convolve(r, carry):
        arrived(*st2(r))

        def one(i, carry):
            u = 2 * i
            xs, ws = [], []
            for j in range(2):
                row, c = (u + j) // 3, lax.rem(u + j, 3)
                xs.append(xb[c, r, row])
                ws.append(sx[r, row, c])
            lre, lim, gre, gim = spectrum(*xs)
            a, d, e, g = spectrum(*ws)
            m = jnp.concatenate(
                [lre * a - lim * d, lre * d + lim * a, gre * e - gim * g, gre * g + gim * e], axis=0
            ).astype(BF)
            v = dot(sig[...], m).astype(BF)
            for j in range(2):
                row, c = (u + j) // 3, lax.rem(u + j, 3)
                fs[r, row, c] = v[:, LANES * j : LANES * j + LANES].reshape(PIECES, 8, LANES)
            return carry

        lax.fori_loop(0, 6, one, 0)
        exchange(*st3(r))
        return carry

    lax.fori_loop(0, 3, convolve, 0)

    def out_copy(r, a):
        dst = (ol, og)[a]
        return pltpu.make_async_copy(
            ob.at[r, a], dst.at[:, 0, :, pl.ds(128 * r, 128), :], out_sem.at[r, a]
        )

    def finish(r, carry):
        arrived(*st3(r))

        def unpack(i, carry):
            for c in range(3):
                x = fr[r, pl.ds(8 * i, 8), :, c].reshape(32, 8, LANES)
                ob[r, :, :, :, pl.ds(32 * i, 32), LANES * c : LANES * c + LANES] = jnp.swapaxes(
                    x, 0, 1
                ).reshape(2, 2, 2, 32, LANES)
            return carry

        lax.fori_loop(0, 4, unpack, 0)
        for a in range(2):
            out_copy(r, a).start()
        return carry

    lax.fori_loop(0, 3, finish, 0)

    for r in range(3):
        for st in (st0, st1, st2, st3):
            stage, part, _, _, span = st(r)
            sent(stage, part, span)

        @pl.when(b < 3)
        def _():
            near_copy(r, 0, core_id).wait_send()

        @pl.when(b > 0)
        def _():
            near_copy(r, 2, core_id).wait_send()

        for a in range(2):
            out_copy(r, a).wait()


def local(lesser_green, greater_green, coulomb_blocks):
    fwd, pol, sig = dft_tables()
    any_spec = pl.BlockSpec(memory_space=pl.ANY)
    out = jax.ShapeDtypeStruct(lesser_green.shape, BF)
    tile = (8, LANES)
    dma = pltpu.SemaphoreType.DMA
    return pl.pallas_call(
        kernel,
        out_shape=(out, out),
        in_specs=[any_spec] * 6,
        out_specs=(any_spec, any_spec),
        scratch_shapes=[
            pltpu.VMEM((3, 2, 2, 2, ROWS, LANES), BF),
            pltpu.VMEM((3, 3, PIECES, 4) + tile, BF),
            pltpu.VMEM((3, 3, 4, PIECES) + tile, BF),
            pltpu.VMEM((3, 3, 4, PIECES) + tile, BF),
            pltpu.VMEM((3, 3, PIECES, 4) + tile, BF),
            pltpu.VMEM((3, 3, 8, ROWS, LANES), BF),
            pltpu.VMEM((3, 3, 4, 128, 2 * ROWS), BF),
            pltpu.VMEM((3, 8, 128, LANES), BF),
            pltpu.VMEM((3, PIECES, 4, 3) + tile, BF),
            pltpu.VMEM((3, 4, 3, PIECES) + tile, BF),
            pltpu.VMEM((3, 4, 3, PIECES) + tile, BF),
            pltpu.VMEM((3, PIECES, 4, 3) + tile, BF),
            pltpu.VMEM((3, 2, 2, 2, 128, ROWS), BF),
            pltpu.VMEM((3, ROWS, 2 * ROWS), BF),
            pltpu.VMEM((3, 2 * ROWS, 2 * ROWS), BF),
            pltpu.VMEM((4 * LENGTH, 4 * NE), BF),
            pltpu.VMEM((4 * NE, 2 * LENGTH), BF),
            pltpu.VMEM((4 * NE, 4 * LENGTH), BF),
            dma((3, 2)), dma((9,)), dma((4, 3)), dma((4, 3)), dma((4, 3)), dma((3, 3)), dma((3, 3)),
            dma((3, 2)),
        ],
        compiler_params=pltpu.CompilerParams(
            collective_id=0, has_side_effects=True, vmem_limit_bytes=66_000_000
        ),
        name="gw",
    )(lesser_green, greater_green, coulomb_blocks, fwd, pol, sig)


def solution(mesh):
    return jax.shard_map(
        local,
        mesh=mesh,
        in_specs=(
            P("energy", "blk", None, None, None),
            P("energy", "blk", None, None, None),
            P("blk", None, None, None, None),
        ),
        out_specs=(P("energy", "blk", None, None, None), P("energy", "blk", None, None, None)),
        check_vma=False,
    )
```

time: 297 us -> 136 us (0.46); the launches traced: 293 us -> 135 us
  Pallas kernels: 0 us -> 131 us
  matrix products: 84.1 us -> 0 us
  waiting for transfers between devices: 81.5 us -> 0 us
  starting transfers between devices: 61.2 us -> 0 us
  local copies, waits for them, and re-layouts: 61.9 us -> 3.51 us
    pallas_call x0 -> x1, Pallas kernels: none -> 131 us  [local(): pl.pallas_call(kernel, out_shape=(out, out), in_specs=[any_spec] * 6, out...]
    dot_general x70 -> x0, matrix products: 84.1 us -> none  [the longest x16 23.6 us: apply_split(): jnp.einsum(form, table_pair[1], data, preferred_element_type=jnp.float32)]
    all_to_all x8 -> x0, waiting for transfers between devices: 63.3 us -> none  [the longest x2 28.8 us: to_elements(): lax.all_to_all(pair[0], 'energy', split_axis=3, concat_axis=0, tiled=True)]
    all_to_all x8 -> x0, starting transfers between devices: 49.7 us -> none  [the longest x4 26.6 us: to_energies(): lax.all_to_all(for_sending(flat), 'energy', split_axis=0, concat_axis=3,...]
    another operation x16 -> x0, local copies, waits for them, and re-layouts: 29.4 us -> none  [the longest x12 21 us: join_parts(): return jnp.stack([values[0], values[1]], axis=3).astype(jnp.bfloat16)]
    ppermute x2 -> x0, waiting for transfers between devices: 18.1 us -> none  [the longest x1 18.1 us: extended(): lax.ppermute(lax.slice_in_dim(block, block.shape[dim] - width, None, axis...]
    unnamed x44 -> x4, local copies, waits for them, and re-layouts: 15.7 us -> 3.51 us
    ppermute x2 -> x0, starting transfers between devices: 11.6 us -> none  [the longest x1 6.29 us: extended(): lax.ppermute(lax.slice_in_dim(block, 0, width, axis=dim), axis, backward)]
  transfers between devices with their start and end apart: 10 -> 0, of which waited for: 8 -> 0; matrix products, arithmetic and copies ran while one was open for 23% -> 0% of each run, Pallas kernels for 0% -> 0%
where the time goes in v1:
time: 136 us; the launch traced here: 135 us
  Pallas kernels  131 us (96%)
  local copies, waits for them, and re-layouts  3.51 us (3%)
    pallas_call x1, Pallas kernels, local(): pl.pallas_call(kernel, out_shape=(out, out), in_specs=[any_spec] * 6, out...  131 us
    unnamed x4, local copies, waits for them, and re-layouts  3.51 us

profile of v1, /device:TPU:1, one launch (start us, length us, event | category | flops | bytes accessed | tf_op | source)
XLA Modules:
  0.0 134.7 jit_solution(14098133165186617174)
XLA Ops:
  0.6 130.5 %gw.1 = (bf16[2,1,2,384,384]{4,3,2,1,0:T(8,128)(2,1)}, bf16[2,1,2,384,384]{4,3,2,1,0:T(8,128)(2,1)}) custom-call(bf16[2,1,2,384,384]{4,3,2,1,0:T(8,128)(2,1)} %lg.1, bf16[2,1,2,384,384]{4,3,2,1,0:T(8,128)(2,1)} %gg.1, bf16[1,3,2,384,384]{4,3,2,1,0:T(8,128)(2,1)} %cb.1, bf16[512,256]{1,0:T(8,128)(2,1)} %constant.12.fwd_h, bf16[256,256]{1,0:T(8,128)(2,1)} %constant.13.pol_h, ...), custom_call_target="tpu_custom_call" | custom-call | tf_op jit(solution)/shard_map/gw/pallas_call | solution.py:394
  131.1 0.0 copy-start
  131.2 2.5 %copy.10 = bf16[2,1,2,384,384]{4,3,2,1,0:T(8,128)(2,1)} copy(bf16[2,1,2,384,384]{4,3,2,1,0:T(8,128)(2,1)} %get-tuple-element.4) | data formatting | bytes 2359296
  133.7 0.0 copy-done
  133.7 1.0 copy.11
Async XLA Ops:
  131.1 2.5 %copy-start = (bf16[2,1,2,384,384]{4,3,2,1,0:T(8,128)(2,1)S(1)}, bf16[2,1,2,384,384]{4,3,2,1,0:T(8,128)(2,1)}, u32[]{:S(2)}) copy-start(bf16[2,1,2,384,384]{4,3,2,1,0:T(8,128)(2,1)} %get-tuple-element.5) | copy-start | bytes 3538948

commit v2 on v1

v2 whole, which is shorter than its diff:
```python
import functools
import math

import numpy as np
import jax
import jax.numpy as jnp
from jax import lax
from jax.experimental import pallas as pl
from jax.experimental.pallas import tpu as pltpu
from jax.sharding import PartitionSpec as P

MESH = pl.DeviceIdType.MESH
BF = jnp.bfloat16
F32 = jnp.float32
PIECES = 32
ROWS = 384
LANES = 128
NE = 64
LENGTH = 2 * NE


def dft_tables():
    f = np.arange(LENGTH)[:, None]
    e = np.arange(NE)[None, :]
    angle = 2.0 * math.pi / LENGTH * (f * e % LENGTH)
    cos, sin = np.cos(angle), np.sin(angle)
    fwd = np.zeros((2, 2, LENGTH, PIECES, 2, 2, 2))
    cs = cos.reshape(LENGTH, PIECES, 2)
    sn = sin.reshape(LENGTH, PIECES, 2)
    for k in range(2):
        fwd[k, 0, :, :, k, :, 0] = cs
        fwd[k, 0, :, :, k, :, 1] = sn
        fwd[k, 1, :, :, k, :, 0] = -sn
        fwd[k, 1, :, :, k, :, 1] = cs
    ct = cs.transpose(1, 2, 0)
    st = sn.transpose(1, 2, 0)
    scale = 1.0 / (math.sqrt(NE) * LENGTH)
    pol = np.zeros((2, PIECES, 2, 2, 2, 2, 2, LENGTH))
    for h in range(2):
        pol[0, :, h, :, 0, h, 0] = ct
        pol[0, :, h, :, 0, h, 1] = -st
        pol[0, :, h, :, 1, h, 0] = st
        pol[0, :, h, :, 1, h, 1] = ct
        pol[1, :, h, :, 0, h, 0] = ct
        pol[1, :, h, :, 0, h, 1] = st
        pol[1, :, h, :, 1, h, 0] = st
        pol[1, :, h, :, 1, h, 1] = -ct
    sig = np.zeros((PIECES, 2, 2, 2, 2, 2, LENGTH))
    for k in range(2):
        sig[:, k, :, 0, k, 0] = ct
        sig[:, k, :, 0, k, 1] = -st
        sig[:, k, :, 1, k, 0] = st
        sig[:, k, :, 1, k, 1] = ct
    as_bf = lambda a, m, n: jnp.asarray(a.reshape(m, n).astype(np.float32)).astype(BF)
    return (
        as_bf(fwd, 4 * LENGTH, 4 * NE),
        as_bf(-scale * pol, 8 * NE, 4 * LENGTH),
        as_bf(scale * sig, 4 * NE, 4 * LENGTH),
    )


def mirror(t):
    return (t // 8) * 8 + (1 - lax.rem(t // 4, 2)) * 4 + lax.rem(t, 4)


def dot(a, b):
    return jnp.dot(a, b, preferred_element_type=F32)


def kernel(
    lg, gg, cb, fwd_h, pol_h, sig_h, ol, og,
    gin, s0, xb, ps, pr, p3, lf, sc, ss, sx, fs, fr, ob, cc, rr, fwd, pol, sig,
    in_sem, tab_sem, self_sem, send_sem, recv_sem, near_send, near_recv, out_sem,
):
    me = lax.axis_index("energy")
    b = lax.axis_index("blk")
    upper = b >= 2
    even = lax.rem(b, 2) == 0
    my = me // 8
    mz = lax.rem(me // 4, 2)
    mx = lax.rem(me, 4)

    def lag_of(t):
        return jnp.where(upper, mirror(t), t)

    my_lag = lag_of(me)
    inner = jnp.logical_or(b == 1, b == 2)
    core_id = {"energy": me, "blk": b + 1 - 2 * lax.rem(b, 2)}
    cross_id = {"energy": mirror(me), "blk": 3 - b}

    def target(k):
        dz = lax.rem(k, 2)
        dx = lax.rem(k // 2, 4)
        dy = lax.rem(k // 8 + dx, 4)
        return lax.rem(my + dy, 4) * 8 + lax.rem(mz + dz, 2) * 4 + lax.rem(mx + dx, 4)

    def g_copy(c, a):
        src = (lg, gg)[a]
        return pltpu.make_async_copy(
            src.at[:, 0, :, :, pl.ds(LANES * c, LANES)], gin.at[c, a], in_sem.at[c, a]
        )

    for c in range(3):
        for a in range(2):
            g_copy(c, a).start()
    tables = [
        pltpu.make_async_copy(fwd_h, fwd, tab_sem.at[0]),
        pltpu.make_async_copy(pol_h, pol, tab_sem.at[1]),
        pltpu.make_async_copy(sig_h, sig, tab_sem.at[2]),
    ]
    for o in range(3):
        for r in range(2):
            tables.append(
                pltpu.make_async_copy(
                    cb.at[0, o, r], cc.at[o, :, pl.ds(ROWS * r, ROWS)], tab_sem.at[3 + 2 * o + r]
                )
            )
    for copy in tables:
        copy.start()

    barrier = pltpu.get_barrier_semaphore()

    def greet(k, carry):
        pl.semaphore_signal(
            barrier, inc=1, device_id={"energy": target(k), "blk": b}, device_id_type=MESH
        )
        return carry

    lax.fori_loop(1, PIECES, greet, 0)
    pl.semaphore_signal(barrier, inc=1, device_id=core_id, device_id_type=MESH)

    @pl.when(inner)
    def _():
        pl.semaphore_signal(barrier, inc=1, device_id=cross_id, device_id_type=MESH)

    def exchange(stage, part, source, dest, span):
        def go(k, carry):
            t = target(k)
            pltpu.make_async_remote_copy(
                src_ref=source(t), dst_ref=dest(), send_sem=send_sem.at[stage, part],
                recv_sem=recv_sem.at[stage, part], device_id={"energy": t, "blk": b},
                device_id_type=MESH,
            ).start()
            return carry

        lax.fori_loop(1, PIECES, go, 0)
        pltpu.make_async_copy(source(me), dest(), self_sem.at[stage, part]).start()

    def arrived(stage, part, source, dest, span):
        pltpu.make_async_copy(span, span, recv_sem.at[stage, part]).wait()
        pltpu.make_async_copy(source(me), dest(), self_sem.at[stage, part]).wait()

    def sent(stage, part, span):
        pltpu.make_async_copy(span, span, send_sem.at[stage, part]).wait()

    others = pl.ds(0, PIECES - 1)

    def st0(c):
        return (
            0, c, lambda t: s0.at[c, :, :, t], lambda: xb.at[c, :, :, :, me],
            xb.at[c, :, :, :, others],
        )

    def st1(k, c):
        return (
            1, 3 * k + c, lambda t: ps.at[k, c, :, :, lag_of(t)], lambda: pr.at[k, c, :, me],
            pr.at[k, c, :, others],
        )

    def st2(k, r):
        return (
            2, 3 * k + r, lambda t: ss.at[k, r, t], lambda: sx.at[k, r, :, :, my_lag],
            sx.at[k, r, :, :, others],
        )

    def st3(k, r):
        return (
            3, 3 * k + r, lambda t: fs.at[k, r, :, :, t], lambda: fr.at[k, r, me],
            fr.at[k, r, others],
        )

    for c in range(3):
        for a in range(2):
            g_copy(c, a).wait()

        def pack(i, carry):
            r, h = i // 2, lax.rem(i, 2)
            for j in range(2):
                x = gin[c, :, :, :, pl.ds(64 * i + 32 * j, 32), :].reshape(8, 32, LANES)
                s0[c, r, h, 16 * j : 16 * j + 16] = jnp.swapaxes(x, 0, 1).reshape(16, 2, 8, LANES)
            return carry

        lax.fori_loop(0, 6, pack, 0)
        if c == 0:
            pl.semaphore_wait(barrier, jnp.where(inner, PIECES + 1, PIECES))
        exchange(*st0(c))

    for copy in tables:
        copy.wait()
    for o in range(3):
        cre = cc[o, :, :ROWS].T
        cim = cc[o, :, ROWS:].T
        rr[o, :ROWS, :ROWS] = cre
        rr[o, ROWS:, ROWS:] = cre
        rr[o, ROWS:, :ROWS] = cim
        rr[o, :ROWS, ROWS:] = -cim

    @pl.when(b == 0)
    def _():
        lf[:, :, :, :, : 2 * ROWS] = jnp.zeros(lf.shape[:4] + (2 * ROWS,), BF)

    @pl.when(b == 3)
    def _():
        lf[:, :, :, :, 4 * ROWS :] = jnp.zeros(lf.shape[:4] + (2 * ROWS,), BF)

    n = LENGTH

    def side(x0, x1):
        return jnp.concatenate([x0.reshape(256, LANES), x1.reshape(256, LANES)], axis=1)

    def polarize(c, carry):
        arrived(*st0(c))

        def one(r, carry):
            cross = []
            for h in range(2):
                y = dot(fwd[...], side(xb[c, r, h, 0], xb[c, r, h, 1]))
                lre, lim, gre, gim = y[:n], y[n : 2 * n], y[2 * n : 3 * n], y[3 * n :]
                cross += [lre * gre + lim * gim, lim * gre - lre * gim]
            p = dot(pol[...], jnp.concatenate(cross, axis=0).astype(BF)).astype(BF)
            for k in range(2):
                for i in range(2):
                    ps[k, c, r, i] = p[
                        256 * k : 256 * k + 256, LANES * i : LANES * i + LANES
                    ].reshape(PIECES, 8, LANES)
            return carry

        lax.fori_loop(0, 3, one, 0, unroll=True)
        exchange(*st1(0, c))
        return carry

    lax.fori_loop(0, 3, polarize, 0)

    def second(c, carry):
        exchange(*st1(1, c))
        return carry

    lax.fori_loop(0, 3, second, 0)

    def near_copy(k, c, slot, device):
        return pltpu.make_async_remote_copy(
            src_ref=p3.at[k, 1, c], dst_ref=p3.at[k, slot, c], send_sem=near_send.at[k, slot, c],
            recv_sem=near_recv.at[k, slot, c], device_id=device, device_id_type=MESH,
        )

    def left(k, o, c):
        for q in range(2):
            pre = p3[k, o, c, 2 * q].reshape(ROWS, LANES)
            pim = p3[k, o, c, 2 * q + 1].reshape(ROWS, LANES)
            rhs = jnp.concatenate(
                [jnp.concatenate([pre, pim], axis=1), jnp.concatenate([-pim, pre], axis=1)], axis=0
            )
            v = dot(cc[o], rhs).astype(BF)
            for r in range(3):
                for p in range(2):
                    at = 2 * ROWS * o + ROWS * p + LANES * c
                    lf[k, r, q, :, at : at + LANES] = v[
                        128 * r : 128 * r + 128, LANES * p : LANES * p + LANES
                    ]

    def congruence(k, carry):
        for c in range(3):
            arrived(*st1(k, c))
            for r in range(3):
                for j in range(2):
                    x = pr[k, c, r, 16 * j : 16 * j + 16].reshape(32, 8, LANES)
                    x = jnp.swapaxes(x, 0, 1)
                    for h in range(2):
                        p3[k, 1, c, :, r, h, 32 * j : 32 * j + 32, :] = x[4 * h : 4 * h + 4]

            @pl.when(b < 3)
            def _():
                dev = {"energy": jnp.where(even, me, mirror(me)), "blk": b + 1}
                near_copy(k, c, 0, dev).start()

            @pl.when(b > 0)
            def _():
                dev = {"energy": jnp.where(even, mirror(me), me), "blk": b - 1}
                near_copy(k, c, 2, dev).start()

            left(k, 1, c)

        for c in range(3):
            @pl.when(b > 0)
            def _():
                near_copy(k, c, 0, core_id).wait_recv()
                left(k, 0, c)

            @pl.when(b < 3)
            def _():
                near_copy(k, c, 2, core_id).wait_recv()
                left(k, 2, c)

        for m in range(3):
            v = dot(
                lf[k].reshape(6 * 128, 6 * ROWS),
                rr[:, :, 256 * m : 256 * m + 256].reshape(6 * ROWS, 256),
            ).astype(BF)
            for h in range(2):
                part, c = divmod(2 * m + h, 3)
                for r in range(3):
                    for q in range(2):
                        at = 256 * r + 128 * q
                        sc[c, 2 * q + part, r] = v[
                            at : at + 128, LANES * h : LANES * h + LANES
                        ].reshape(2, 64, LANES)

        def send(r, carry):
            for c in range(3):
                for j in range(2):
                    x = jnp.concatenate(
                        [sc[c, :, r, h, 32 * j : 32 * j + 32, :] for h in range(2)], axis=0
                    )
                    ss[k, r, 16 * j : 16 * j + 16, :, c] = jnp.swapaxes(x, 0, 1).reshape(
                        16, 2, 8, LANES
                    )
            exchange(*st2(k, r))
            return carry

        lax.fori_loop(0, 3, send, 0)
        return carry

    lax.fori_loop(0, 2, congruence, 0)

    def convolve(m, carry):
        k, r = m // 3, lax.rem(m, 3)
        arrived(*st2(k, r))
        half = fwd[pl.ds(pl.multiple_of(256 * k, 256), 256), :]

        def one(c, carry):
            w = dot(fwd[...], side(sx[k, r, 0, c], sx[k, r, 1, c]))
            prod = []
            for h in range(2):
                g = dot(half, side(xb[c, r, h, 0], xb[c, r, h, 1]))
                gre, gim = g[:n], g[n:]
                wre, wim = w[2 * n * h : 2 * n * h + n], w[2 * n * h + n : 2 * n * h + 2 * n]
                prod += [gre * wre - gim * wim, gre * wim + gim * wre]
            v = dot(sig[...], jnp.concatenate(prod, axis=0).astype(BF)).astype(BF)
            for i in range(2):
                fs[k, r, i, c] = v[:, LANES * i : LANES * i + LANES].reshape(PIECES, 8, LANES)
            return carry

        lax.fori_loop(0, 3, one, 0, unroll=True)
        exchange(*st3(k, r))
        return carry

    lax.fori_loop(0, 6, convolve, 0)

    def out_copy(k, r):
        dst = (ol, og)[k]
        return pltpu.make_async_copy(
            ob.at[k, r], dst.at[:, 0, :, pl.ds(128 * r, 128), :], out_sem.at[k, r]
        )

    for k in range(2):

        def finish(r, carry):
            arrived(*st3(k, r))
            for c in range(3):
                for j in range(2):
                    x = fr[k, r, 16 * j : 16 * j + 16, :, c].reshape(32, 8, LANES)
                    x = jnp.swapaxes(x, 0, 1)
                    for h in range(2):
                        at = 64 * h + 32 * j
                        ob[k, r, :, :, at : at + 32, LANES * c : LANES * c + LANES] = x[
                            4 * h : 4 * h + 4
                        ].reshape(2, 2, 32, LANES)
            out_copy(k, r).start()
            return carry

        lax.fori_loop(0, 3, finish, 0)

    for r in range(3):
        sent(*[st0(r)[i] for i in (0, 1, 4)])

    def drain(m, carry):
        k, r = m // 3, lax.rem(m, 3)
        for st in (st1, st2, st3):
            sent(*[st(k, r)[i] for i in (0, 1, 4)])

        @pl.when(b < 3)
        def _():
            near_copy(k, r, 0, core_id).wait_send()

        @pl.when(b > 0)
        def _():
            near_copy(k, r, 2, core_id).wait_send()

        return carry

    lax.fori_loop(0, 6, drain, 0)
    for k in range(2):
        for r in range(3):
            out_copy(k, r).wait()


def local(lesser_green, greater_green, coulomb_blocks):
    fwd, pol, sig = dft_tables()
    any_spec = pl.BlockSpec(memory_space=pl.ANY)
    out = jax.ShapeDtypeStruct(lesser_green.shape, BF)
    tile = (8, LANES)
    dma = pltpu.SemaphoreType.DMA
    return pl.pallas_call(
        kernel,
        out_shape=(out, out),
        in_specs=[any_spec] * 6,
        out_specs=(any_spec, any_spec),
        scratch_shapes=[
            pltpu.VMEM((3, 2, 2, 2, ROWS, LANES), BF),
            pltpu.VMEM((3, 3, 2, PIECES, 2) + tile, BF),
            pltpu.VMEM((3, 3, 2, 2, PIECES) + tile, BF),
            pltpu.VMEM((2, 3, 3, 2, PIECES) + tile, BF),
            pltpu.VMEM((2, 3, 3, PIECES, 2) + tile, BF),
            pltpu.VMEM((2, 3, 3, 4, 3, 2, 64, LANES), BF),
            pltpu.VMEM((2, 3, 2, 128, 6 * ROWS), BF),
            pltpu.VMEM((3, 4, 3, 2, 64, LANES), BF),
            pltpu.VMEM((2, 3, PIECES, 2, 3) + tile, BF),
            pltpu.VMEM((2, 3, 2, 3, PIECES) + tile, BF),
            pltpu.VMEM((2, 3, 2, 3, PIECES) + tile, BF),
            pltpu.VMEM((2, 3, PIECES, 2, 3) + tile, BF),
            pltpu.VMEM((2, 3, 2, 2, 128, ROWS), BF),
            pltpu.VMEM((3, ROWS, 2 * ROWS), BF),
            pltpu.VMEM((3, 2 * ROWS, 2 * ROWS), BF),
            pltpu.VMEM((4 * LENGTH, 4 * NE), BF),
            pltpu.VMEM((8 * NE, 4 * LENGTH), BF),
            pltpu.VMEM((4 * NE, 4 * LENGTH), BF),
            dma((3, 2)), dma((9,)), dma((4, 6)), dma((4, 6)), dma((4, 6)), dma((2, 3, 3)),
            dma((2, 3, 3)), dma((2, 3)),
        ],
        compiler_params=pltpu.CompilerParams(
            collective_id=0, has_side_effects=True, vmem_limit_bytes=66_000_000
        ),
        name="gw",
    )(lesser_green, greater_green, coulomb_blocks, fwd, pol, sig)


def solution(mesh):
    return jax.shard_map(
        local,
        mesh=mesh,
        in_specs=(
            P("energy", "blk", None, None, None),
            P("energy", "blk", None, None, None),
            P("blk", None, None, None, None),
        ),
        out_specs=(P("energy", "blk", None, None, None), P("energy", "blk", None, None, None)),
        check_vma=False,
    )
```

time: 136 us -> 124 us (0.912)
  Pallas kernels: 131 us -> 120 us
    pallas_call x1, Pallas kernels: 131 us -> 120 us  [local(): pl.pallas_call(kernel, out_shape=(out, out), in_specs=[any_spec] * 6, out...]
where the time goes in v2:
time: 124 us
  Pallas kernels  120 us (97%)
  local copies, waits for them, and re-layouts  3.51 us (3%)
    pallas_call x1, Pallas kernels, local(): pl.pallas_call(kernel, out_shape=(out, out), in_specs=[any_spec] * 6, out...  120 us
    unnamed x4, local copies, waits for them, and re-layouts  3.51 us

profile of v2, /device:TPU:1, one launch (start us, length us, event | category | flops | bytes accessed | tf_op | source)
XLA Modules:
  0.0 124.0 jit_solution(14284163809852636360)
XLA Ops:
  0.6 119.9 %gw.1 = (bf16[2,1,2,384,384]{4,3,2,1,0:T(8,128)(2,1)}, bf16[2,1,2,384,384]{4,3,2,1,0:T(8,128)(2,1)}) custom-call(bf16[2,1,2,384,384]{4,3,2,1,0:T(8,128)(2,1)} %lg.1, bf16[2,1,2,384,384]{4,3,2,1,0:T(8,128)(2,1)} %gg.1, bf16[1,3,2,384,384]{4,3,2,1,0:T(8,128)(2,1)} %cb.1, bf16[512,256]{1,0:T(8,128)(2,1)} %constant.12.fwd_h, bf16[512,512]{1,0:T(8,128)(2,1)} %constant.13.pol_h, ...), custom_call_target="tpu_custom_call" | custom-call | tf_op jit(solution)/shard_map/gw/pallas_call | solution.py:413
  120.5 0.0 copy-start
  120.5 2.5 %copy.10 = bf16[2,1,2,384,384]{4,3,2,1,0:T(8,128)(2,1)} copy(bf16[2,1,2,384,384]{4,3,2,1,0:T(8,128)(2,1)} %get-tuple-element.4) | data formatting | bytes 2359296
  123.0 0.0 copy-done
  123.0 1.0 copy.11
Async XLA Ops:
  120.5 2.5 %copy-start = (bf16[2,1,2,384,384]{4,3,2,1,0:T(8,128)(2,1)S(1)}, bf16[2,1,2,384,384]{4,3,2,1,0:T(8,128)(2,1)}, u32[]{:S(2)}) copy-start(bf16[2,1,2,384,384]{4,3,2,1,0:T(8,128)(2,1)} %get-tuple-element.5) | copy-start | bytes 3538948

commit v3 on v2

--- a/solution.py
+++ b/solution.py
@@ -69,7 +69,7 @@
 
 def kernel(
     lg, gg, cb, fwd_h, pol_h, sig_h, ol, og,
-    gin, s0, xb, ps, pr, p3, lf, sc, ss, sx, fs, fr, ob, cc, rr, fwd, pol, sig,
+    gin, s0, xb, ps, pr, p3, lf, acc, sc, ss, sx, fs, fr, ob, cc, rr, fwd, pol, sig,
     in_sem, tab_sem, self_sem, send_sem, recv_sem, near_send, near_recv, out_sem,
 ):
     me = lax.axis_index("energy")
@@ -79,20 +79,33 @@
     my = me // 8
     mz = lax.rem(me // 4, 2)
     mx = lax.rem(me, 4)
-
-    def lag_of(t):
-        return jnp.where(upper, mirror(t), t)
-
-    my_lag = lag_of(me)
     inner = jnp.logical_or(b == 1, b == 2)
     core_id = {"energy": me, "blk": b + 1 - 2 * lax.rem(b, 2)}
     cross_id = {"energy": mirror(me), "blk": 3 - b}
-
-    def target(k):
-        dz = lax.rem(k, 2)
-        dx = lax.rem(k // 2, 4)
-        dy = lax.rem(k // 8 + dx, 4)
-        return lax.rem(my + dy, 4) * 8 + lax.rem(mz + dz, 2) * 4 + lax.rem(mx + dx, 4)
+    core_o = jnp.where(even, 2, 0)
+    offsets = (1, core_o, 2 - core_o)
+
+    ys = [8 * lax.rem(my + d, 4) for d in range(4)]
+    xs = [lax.rem(mx + d, 4) for d in range(4)]
+    zs = [4 * mz, 4 - 4 * mz]
+    lag_zs = [jnp.where(upper, 4 - z, z) for z in zs]
+    my_lag = 8 * my + lag_zs[0] + mx
+    peers = []
+    for k in range(PIECES):
+        dz, dx = k % 2, k // 2 % 4
+        dy = (k // 8 + dx) % 4
+        peers.append((ys[dy] + zs[dz] + xs[dx], ys[dy] + lag_zs[dz] + xs[dx]))
+
+    barrier = pltpu.get_barrier_semaphore()
+    for t, _ in reversed(peers[1:]):
+        pl.semaphore_signal(
+            barrier, inc=1, device_id={"energy": t, "blk": b}, device_id_type=MESH
+        )
+    pl.semaphore_signal(barrier, inc=1, device_id=core_id, device_id_type=MESH)
+
+    @pl.when(inner)
+    def _():
+        pl.semaphore_signal(barrier, inc=1, device_id=cross_id, device_id_type=MESH)
 
     def g_copy(c, a):
         src = (lg, gg)[a]
@@ -100,9 +113,8 @@
             src.at[:, 0, :, :, pl.ds(LANES * c, LANES)], gin.at[c, a], in_sem.at[c, a]
         )
 
-    for c in range(3):
-        for a in range(2):
-            g_copy(c, a).start()
+    for a in range(2):
+        g_copy(0, a).start()
     tables = [
         pltpu.make_async_copy(fwd_h, fwd, tab_sem.at[0]),
         pltpu.make_async_copy(pol_h, pol, tab_sem.at[1]),
@@ -112,43 +124,24 @@
         for r in range(2):
             tables.append(
                 pltpu.make_async_copy(
-                    cb.at[0, o, r], cc.at[o, :, pl.ds(ROWS * r, ROWS)], tab_sem.at[3 + 2 * o + r]
+                    cb.at[0, offsets[o], r],
+                    cc.at[o, :, pl.ds(ROWS * r, ROWS)],
+                    tab_sem.at[3 + 2 * o + r],
                 )
             )
-    for copy in tables:
-        copy.start()
-
-    barrier = pltpu.get_barrier_semaphore()
-
-    def greet(k, carry):
-        pl.semaphore_signal(
-            barrier, inc=1, device_id={"energy": target(k), "blk": b}, device_id_type=MESH
-        )
-        return carry
-
-    lax.fori_loop(1, PIECES, greet, 0)
-    pl.semaphore_signal(barrier, inc=1, device_id=core_id, device_id_type=MESH)
-
-    @pl.when(inner)
-    def _():
-        pl.semaphore_signal(barrier, inc=1, device_id=cross_id, device_id_type=MESH)
 
     def exchange(stage, part, source, dest, span):
-        def go(k, carry):
-            t = target(k)
+        for t, lag in peers[1:]:
             pltpu.make_async_remote_copy(
-                src_ref=source(t), dst_ref=dest(), send_sem=send_sem.at[stage, part],
+                src_ref=source(t, lag), dst_ref=dest(), send_sem=send_sem.at[stage, part],
                 recv_sem=recv_sem.at[stage, part], device_id={"energy": t, "blk": b},
                 device_id_type=MESH,
             ).start()
-            return carry
-
-        lax.fori_loop(1, PIECES, go, 0)
-        pltpu.make_async_copy(source(me), dest(), self_sem.at[stage, part]).start()
+        pltpu.make_async_copy(source(me, my_lag), dest(), self_sem.at[stage, part]).start()
 
     def arrived(stage, part, source, dest, span):
         pltpu.make_async_copy(span, span, recv_sem.at[stage, part]).wait()
-        pltpu.make_async_copy(source(me), dest(), self_sem.at[stage, part]).wait()
+        pltpu.make_async_copy(source(me, my_lag), dest(), self_sem.at[stage, part]).wait()
 
     def sent(stage, part, span):
         pltpu.make_async_copy(span, span, send_sem.at[stage, part]).wait()
@@ -157,31 +150,35 @@
 
     def st0(c):
         return (
-            0, c, lambda t: s0.at[c, :, :, t], lambda: xb.at[c, :, :, :, me],
+            0, c, lambda t, lag: s0.at[c, :, :, t], lambda: xb.at[c, :, :, :, me],
             xb.at[c, :, :, :, others],
         )
 
     def st1(k, c):
         return (
-            1, 3 * k + c, lambda t: ps.at[k, c, :, :, lag_of(t)], lambda: pr.at[k, c, :, me],
+            1, 3 * k + c, lambda t, lag: ps.at[k, c, :, :, lag], lambda: pr.at[k, c, :, me],
             pr.at[k, c, :, others],
         )
 
     def st2(k, r):
         return (
-            2, 3 * k + r, lambda t: ss.at[k, r, t], lambda: sx.at[k, r, :, :, my_lag],
+            2, 3 * k + r, lambda t, lag: ss.at[k, r, t], lambda: sx.at[k, r, :, :, my_lag],
             sx.at[k, r, :, :, others],
         )
 
     def st3(k, r):
         return (
-            3, 3 * k + r, lambda t: fs.at[k, r, :, :, t], lambda: fr.at[k, r, me],
+            3, 3 * k + r, lambda t, lag: fs.at[k, r, :, :, t], lambda: fr.at[k, r, me],
             fr.at[k, r, others],
         )
 
     for c in range(3):
         for a in range(2):
             g_copy(c, a).wait()
+        if c == 0:
+            for d in range(1, 3):
+                for a in range(2):
+                    g_copy(d, a).start()
 
         def pack(i, carry):
             r, h = i // 2, lax.rem(i, 2)
@@ -195,6 +192,8 @@
             pl.semaphore_wait(barrier, jnp.where(inner, PIECES + 1, PIECES))
         exchange(*st0(c))
 
+    for copy in tables:
+        copy.start()
     for copy in tables:
         copy.wait()
     for o in range(3):
@@ -204,14 +203,6 @@
         rr[o, ROWS:, ROWS:] = cre
         rr[o, ROWS:, :ROWS] = cim
         rr[o, :ROWS, ROWS:] = -cim
-
-    @pl.when(b == 0)
-    def _():
-        lf[:, :, :, :, : 2 * ROWS] = jnp.zeros(lf.shape[:4] + (2 * ROWS,), BF)
-
-    @pl.when(b == 3)
-    def _():
-        lf[:, :, :, :, 4 * ROWS :] = jnp.zeros(lf.shape[:4] + (2 * ROWS,), BF)
 
     n = LENGTH
 
@@ -241,17 +232,29 @@
 
     lax.fori_loop(0, 3, polarize, 0)
 
-    def second(c, carry):
-        exchange(*st1(1, c))
-        return carry
-
-    lax.fori_loop(0, 3, second, 0)
-
-    def near_copy(k, c, slot, device):
+    exchange(*st1(1, 0))
+
+    def near_copy(k, c, slot):
         return pltpu.make_async_remote_copy(
-            src_ref=p3.at[k, 1, c], dst_ref=p3.at[k, slot, c], send_sem=near_send.at[k, slot, c],
-            recv_sem=near_recv.at[k, slot, c], device_id=device, device_id_type=MESH,
-        )
+            src_ref=p3.at[k, 0, c], dst_ref=p3.at[k, slot, c], send_sem=near_send.at[k, slot, c],
+            recv_sem=near_recv.at[k, slot, c], device_id=core_id if slot == 1 else cross_id,
+            device_id_type=MESH,
+        )
+
+    def unpack(k, c):
+        arrived(*st1(k, c))
+        for r in range(3):
+            for j in range(2):
+                x = pr[k, c, r, 16 * j : 16 * j + 16].reshape(32, 8, LANES)
+                x = jnp.swapaxes(x, 0, 1)
+                for h in range(2):
+                    p3[k, 0, c, :, r, h, 32 * j : 32 * j + 32, :] = x[4 * h : 4 * h + 4]
+
+        @pl.when(inner)
+        def _():
+            near_copy(k, c, 2).start()
+
+        near_copy(k, c, 1).start()
 
     def left(k, o, c):
         for q in range(2):
@@ -261,51 +264,33 @@
                 [jnp.concatenate([pre, pim], axis=1), jnp.concatenate([-pim, pre], axis=1)], axis=0
             )
             v = dot(cc[o], rhs).astype(BF)
-            for r in range(3):
-                for p in range(2):
-                    at = 2 * ROWS * o + ROWS * p + LANES * c
+            for p in range(2):
+                at = 2 * ROWS * o + ROWS * p + LANES * c
+                for r in range(3):
                     lf[k, r, q, :, at : at + LANES] = v[
                         128 * r : 128 * r + 128, LANES * p : LANES * p + LANES
                     ]
 
-    def congruence(k, carry):
-        for c in range(3):
-            arrived(*st1(k, c))
-            for r in range(3):
-                for j in range(2):
-                    x = pr[k, c, r, 16 * j : 16 * j + 16].reshape(32, 8, LANES)
-                    x = jnp.swapaxes(x, 0, 1)
-                    for h in range(2):
-                        p3[k, 1, c, :, r, h, 32 * j : 32 * j + 32, :] = x[4 * h : 4 * h + 4]
-
-            @pl.when(b < 3)
-            def _():
-                dev = {"energy": jnp.where(even, me, mirror(me)), "blk": b + 1}
-                near_copy(k, c, 0, dev).start()
-
-            @pl.when(b > 0)
-            def _():
-                dev = {"energy": jnp.where(even, mirror(me), me), "blk": b - 1}
-                near_copy(k, c, 2, dev).start()
-
-            left(k, 1, c)
-
-        for c in range(3):
-            @pl.when(b > 0)
-            def _():
-                near_copy(k, c, 0, core_id).wait_recv()
-                left(k, 0, c)
-
-            @pl.when(b < 3)
-            def _():
-                near_copy(k, c, 2, core_id).wait_recv()
-                left(k, 2, c)
-
+    def beside(k, c):
+        near_copy(k, c, 1).wait_recv()
+        left(k, 1, c)
+
+    def across(k, c):
+        @pl.when(inner)
+        def _():
+            near_copy(k, c, 2).wait_recv()
+            left(k, 2, c)
+
+    def right_near(k):
         for m in range(3):
-            v = dot(
-                lf[k].reshape(6 * 128, 6 * ROWS),
-                rr[:, :, 256 * m : 256 * m + 256].reshape(6 * ROWS, 256),
-            ).astype(BF)
+            acc[:, 256 * m : 256 * m + 256] = dot(
+                lf[k, :, :, :, : 4 * ROWS].reshape(6 * 128, 4 * ROWS),
+                rr[:2, :, 256 * m : 256 * m + 256].reshape(4 * ROWS, 256),
+            )
+
+    def right_far(k):
+        def emit(m, v):
+            v = v.astype(BF)
             for h in range(2):
                 part, c = divmod(2 * m + h, 3)
                 for r in range(3):
@@ -315,22 +300,65 @@
                             at : at + 128, LANES * h : LANES * h + LANES
                         ].reshape(2, 64, LANES)
 
-        def send(r, carry):
-            for c in range(3):
-                for j in range(2):
-                    x = jnp.concatenate(
-                        [sc[c, :, r, h, 32 * j : 32 * j + 32, :] for h in range(2)], axis=0
-                    )
-                    ss[k, r, 16 * j : 16 * j + 16, :, c] = jnp.swapaxes(x, 0, 1).reshape(
-                        16, 2, 8, LANES
-                    )
-            exchange(*st2(k, r))
-            return carry
-
-        lax.fori_loop(0, 3, send, 0)
-        return carry
-
-    lax.fori_loop(0, 2, congruence, 0)
+        @pl.when(inner)
+        def _():
+            for m in range(3):
+                emit(
+                    m,
+                    acc[:, 256 * m : 256 * m + 256]
+                    + dot(
+                        lf[k, :, :, :, 4 * ROWS :].reshape(6 * 128, 2 * ROWS),
+                        rr[2, :, 256 * m : 256 * m + 256],
+                    ),
+                )
+
+        @pl.when(jnp.logical_not(inner))
+        def _():
+            for m in range(3):
+                emit(m, acc[:, 256 * m : 256 * m + 256])
+
+    def send(k, r):
+        for c in range(3):
+            for j in range(2):
+                x = jnp.concatenate(
+                    [sc[c, :, r, h, 32 * j : 32 * j + 32, :] for h in range(2)], axis=0
+                )
+                ss[k, r, 16 * j : 16 * j + 16, :, c] = jnp.swapaxes(x, 0, 1).reshape(
+                    16, 2, 8, LANES
+                )
+        exchange(*st2(k, r))
+
+    unpack(0, 0)
+    exchange(*st1(1, 1))
+    unpack(0, 1)
+    exchange(*st1(1, 2))
+    left(0, 0, 0)
+    left(0, 0, 1)
+    beside(0, 0)
+    unpack(0, 2)
+    left(0, 0, 2)
+    beside(0, 1)
+    beside(0, 2)
+    right_near(0)
+    across(0, 0)
+    unpack(1, 0)
+    across(0, 1)
+    unpack(1, 1)
+    across(0, 2)
+    right_far(0)
+    send(0, 0)
+    send(0, 1)
+    unpack(1, 2)
+    send(0, 2)
+    for c in range(3):
+        left(1, 0, c)
+        beside(1, c)
+    right_near(1)
+    for c in range(3):
+        across(1, c)
+    right_far(1)
+    for r in range(3):
+        send(1, r)
 
     def convolve(m, carry):
         k, r = m // 3, lax.rem(m, 3)
@@ -355,6 +383,19 @@
         return carry
 
     lax.fori_loop(0, 6, convolve, 0)
+
+    for r in range(3):
+        sent(*[st0(r)[i] for i in (0, 1, 4)])
+        for k in range(2):
+            for st in (st1, st2):
+                sent(*[st(k, r)[i] for i in (0, 1, 4)])
+            near_copy(k, r, 1).wait_send()
+
+    @pl.when(inner)
+    def _():
+        for r in range(3):
+            for k in range(2):
+                near_copy(k, r, 2).wait_send()
 
     def out_copy(k, r):
         dst = (ol, og)[k]
@@ -380,25 +421,9 @@
 
         lax.fori_loop(0, 3, finish, 0)
 
-    for r in range(3):
-        sent(*[st0(r)[i] for i in (0, 1, 4)])
-
-    def drain(m, carry):
-        k, r = m // 3, lax.rem(m, 3)
-        for st in (st1, st2, st3):
-            sent(*[st(k, r)[i] for i in (0, 1, 4)])
-
-        @pl.when(b < 3)
-        def _():
-            near_copy(k, r, 0, core_id).wait_send()
-
-        @pl.when(b > 0)
-        def _():
-            near_copy(k, r, 2, core_id).wait_send()
-
-        return carry
-
-    lax.fori_loop(0, 6, drain, 0)
+    for k in range(2):
+        for r in range(3):
+            sent(*[st3(k, r)[i] for i in (0, 1, 4)])
     for k in range(2):
         for r in range(3):
             out_copy(k, r).wait()
@@ -423,6 +448,7 @@
             pltpu.VMEM((2, 3, 3, PIECES, 2) + tile, BF),
             pltpu.VMEM((2, 3, 3, 4, 3, 2, 64, LANES), BF),
             pltpu.VMEM((2, 3, 2, 128, 6 * ROWS), BF),
+            pltpu.VMEM((6 * 128, 2 * ROWS), F32),
             pltpu.VMEM((3, 4, 3, 2, 64, LANES), BF),
             pltpu.VMEM((2, 3, PIECES, 2, 3) + tile, BF),
             pltpu.VMEM((2, 3, 2, 3, PIECES) + tile, BF),

time: 124 us -> 121 us (0.976)
  Pallas kernels: 120 us -> 117 us
    pallas_call x1, Pallas kernels: 120 us -> 117 us  [local(): pl.pallas_call(kernel, out_shape=(out, out), in_specs=[any_spec] * 6, out...]
where the time goes in v3:
time: 121 us
  Pallas kernels  117 us (97%)
  local copies, waits for them, and re-layouts  3.51 us (3%)
    pallas_call x1, Pallas kernels, local(): pl.pallas_call(kernel, out_shape=(out, out), in_specs=[any_spec] * 6, out...  117 us
    unnamed x4, local copies, waits for them, and re-layouts  3.51 us

profile of v3, /device:TPU:1, one launch (start us, length us, event | category | flops | bytes accessed | tf_op | source)
XLA Modules:
  0.0 121.2 jit_solution(6681095962326043014)
XLA Ops:
  0.6 117.1 %gw.1 = (bf16[2,1,2,384,384]{4,3,2,1,0:T(8,128)(2,1)}, bf16[2,1,2,384,384]{4,3,2,1,0:T(8,128)(2,1)}) custom-call(bf16[2,1,2,384,384]{4,3,2,1,0:T(8,128)(2,1)} %lg.1, bf16[2,1,2,384,384]{4,3,2,1,0:T(8,128)(2,1)} %gg.1, bf16[1,3,2,384,384]{4,3,2,1,0:T(8,128)(2,1)} %cb.1, bf16[512,256]{1,0:T(8,128)(2,1)} %constant.12.fwd_h, bf16[512,512]{1,0:T(8,128)(2,1)} %constant.13.pol_h, ...), custom_call_target="tpu_custom_call" | custom-call | tf_op jit(solution)/shard_map/gw/pallas_call | solution.py:438
  117.7 0.0 copy-start
  117.7 2.5 %copy.10 = bf16[2,1,2,384,384]{4,3,2,1,0:T(8,128)(2,1)} copy(bf16[2,1,2,384,384]{4,3,2,1,0:T(8,128)(2,1)} %get-tuple-element.4) | data formatting | bytes 2359296
  120.2 0.0 copy-done
  120.2 1.0 copy.11
Async XLA Ops:
  117.7 2.5 %copy-start = (bf16[2,1,2,384,384]{4,3,2,1,0:T(8,128)(2,1)S(1)}, bf16[2,1,2,384,384]{4,3,2,1,0:T(8,128)(2,1)}, u32[]{:S(2)}) copy-start(bf16[2,1,2,384,384]{4,3,2,1,0:T(8,128)(2,1)} %get-tuple-element.5) | copy-start | bytes 3538948

commit v4 on v3

--- a/solution.py
+++ b/solution.py
@@ -59,6 +59,14 @@
     )
 
 
+def hops(step):
+    dy, dz, dx = step
+    return min(dy, 4 - dy) + dz + min(dx, 4 - dx)
+
+
+STEPS = [((k // 8 + k // 2 % 4) % 4, k % 2, k // 2 % 4) for k in range(PIECES)]
+
+
 def mirror(t):
     return (t // 8) * 8 + (1 - lax.rem(t // 4, 2)) * 4 + lax.rem(t, 4)
 
@@ -68,9 +76,9 @@
 
 
 def kernel(
-    lg, gg, cb, fwd_h, pol_h, sig_h, ol, og,
-    gin, s0, xb, ps, pr, p3, lf, acc, sc, ss, sx, fs, fr, ob, cc, rr, fwd, pol, sig,
-    in_sem, tab_sem, self_sem, send_sem, recv_sem, near_send, near_recv, out_sem,
+    lg, gg, cb, fwd_h, pol_h, sig_h, ob,
+    gin, s0, xb, ps, pr, p3, lf, acc, sc, ss, sx, fs, fr, cc, rr, fwd, pol, sig,
+    in_sem, tab_sem, self_sem, send_sem, recv_sem, near_send, near_recv,
 ):
     me = lax.axis_index("energy")
     b = lax.axis_index("blk")
@@ -91,13 +99,11 @@
     lag_zs = [jnp.where(upper, 4 - z, z) for z in zs]
     my_lag = 8 * my + lag_zs[0] + mx
     peers = []
-    for k in range(PIECES):
-        dz, dx = k % 2, k // 2 % 4
-        dy = (k // 8 + dx) % 4
+    for dy, dz, dx in STEPS[:1] + sorted(STEPS[1:], key=hops, reverse=True):
         peers.append((ys[dy] + zs[dz] + xs[dx], ys[dy] + lag_zs[dz] + xs[dx]))
 
     barrier = pltpu.get_barrier_semaphore()
-    for t, _ in reversed(peers[1:]):
+    for t, _ in peers[1:]:
         pl.semaphore_signal(
             barrier, inc=1, device_id={"energy": t, "blk": b}, device_id_type=MESH
         )
@@ -397,12 +403,6 @@
             for k in range(2):
                 near_copy(k, r, 2).wait_send()
 
-    def out_copy(k, r):
-        dst = (ol, og)[k]
-        return pltpu.make_async_copy(
-            ob.at[k, r], dst.at[:, 0, :, pl.ds(128 * r, 128), :], out_sem.at[k, r]
-        )
-
     for k in range(2):
 
         def finish(r, carry):
@@ -416,7 +416,6 @@
                         ob[k, r, :, :, at : at + 32, LANES * c : LANES * c + LANES] = x[
                             4 * h : 4 * h + 4
                         ].reshape(2, 2, 32, LANES)
-            out_copy(k, r).start()
             return carry
 
         lax.fori_loop(0, 3, finish, 0)
@@ -424,9 +423,20 @@
     for k in range(2):
         for r in range(3):
             sent(*[st3(k, r)[i] for i in (0, 1, 4)])
-    for k in range(2):
-        for r in range(3):
-            out_copy(k, r).wait()
+
+
+def write_out(ob, ol, og, sem):
+    copies = [
+        pltpu.make_async_copy(
+            ob.at[k, r], (ol, og)[k].at[:, 0, :, pl.ds(128 * r, 128), :], sem.at[k, r]
+        )
+        for k in range(2)
+        for r in range(3)
+    ]
+    for copy in copies:
+        copy.start()
+    for copy in copies:
+        copy.wait()
 
 
 def local(lesser_green, greater_green, coulomb_blocks):
@@ -435,11 +445,11 @@
     out = jax.ShapeDtypeStruct(lesser_green.shape, BF)
     tile = (8, LANES)
     dma = pltpu.SemaphoreType.DMA
-    return pl.pallas_call(
+    held = pl.pallas_call(
         kernel,
-        out_shape=(out, out),
+        out_shape=pltpu.VMEM((2, 3, 2, 2, 128, ROWS), BF),
         in_specs=[any_spec] * 6,
-        out_specs=(any_spec, any_spec),
+        out_specs=pl.BlockSpec(memory_space=pltpu.VMEM),
         scratch_shapes=[
             pltpu.VMEM((3, 2, 2, 2, ROWS, LANES), BF),
             pltpu.VMEM((3, 3, 2, PIECES, 2) + tile, BF),
@@ -454,20 +464,28 @@
             pltpu.VMEM((2, 3, 2, 3, PIECES) + tile, BF),
             pltpu.VMEM((2, 3, 2, 3, PIECES) + tile, BF),
             pltpu.VMEM((2, 3, PIECES, 2, 3) + tile, BF),
-            pltpu.VMEM((2, 3, 2, 2, 128, ROWS), BF),
             pltpu.VMEM((3, ROWS, 2 * ROWS), BF),
             pltpu.VMEM((3, 2 * ROWS, 2 * ROWS), BF),
             pltpu.VMEM((4 * LENGTH, 4 * NE), BF),
             pltpu.VMEM((8 * NE, 4 * LENGTH), BF),
             pltpu.VMEM((4 * NE, 4 * LENGTH), BF),
             dma((3, 2)), dma((9,)), dma((4, 6)), dma((4, 6)), dma((4, 6)), dma((2, 3, 3)),
-            dma((2, 3, 3)), dma((2, 3)),
+            dma((2, 3, 3)),
         ],
         compiler_params=pltpu.CompilerParams(
-            collective_id=0, has_side_effects=True, vmem_limit_bytes=66_000_000
+            collective_id=0, has_side_effects=True, vmem_limit_bytes=60_000_000
         ),
         name="gw",
     )(lesser_green, greater_green, coulomb_blocks, fwd, pol, sig)
+    return pl.pallas_call(
+        write_out,
+        out_shape=(out, out),
+        in_specs=[any_spec],
+        out_specs=(any_spec, any_spec),
+        scratch_shapes=[dma((2, 3))],
+        compiler_params=pltpu.CompilerParams(vmem_limit_bytes=1_000_000),
+        name="out",
+    )(held)
 
 
 def solution(mesh):

time: 121 us -> 117 us (0.967)
  local copies, waits for them, and re-layouts: 3.51 us -> 0 us
    unnamed x4 -> x0, local copies, waits for them, and re-layouts: 3.51 us -> none
    pallas_call x1 -> x2, Pallas kernels: 117 us -> 116 us  [the longest x1 114 us: local(): pl.pallas_call(kernel, out_shape=pltpu.VMEM((2, 3, 2, 2, 128, ROWS), BF),...]
where the time goes in v4:
time: 117 us; the launch traced here: 116 us
  Pallas kernels  116 us (99%)
    pallas_call x1, Pallas kernels, local(): pl.pallas_call(kernel, out_shape=pltpu.VMEM((2, 3, 2, 2, 128, ROWS), BF),...  114 us

profile of v4, /device:TPU:1, one launch (start us, length us, event | category | flops | bytes accessed | tf_op | source)
XLA Modules:
  0.0 116.4 jit_solution(4205656499477347714)
XLA Ops:
  0.6 114.1 %gw.1.ob = bf16[2,3,2,2,128,384]{5,4,3,2,1,0:T(8,128)(2,1)S(1)} custom-call(bf16[2,1,2,384,384]{4,3,2,1,0:T(8,128)(2,1)} %lg.1, bf16[2,1,2,384,384]{4,3,2,1,0:T(8,128)(2,1)} %gg.1, bf16[1,3,2,384,384]{4,3,2,1,0:T(8,128)(2,1)} %cb.1, bf16[512,256]{1,0:T(8,128)(2,1)} %constant.12.fwd_h, bf16[512,512]{1,0:T(8,128)(2,1)} %constant.13.pol_h, ...), custom_call_target="tpu_custom_call" | custom-call | tf_op jit(solution)/shard_map/gw/pallas_call | solution.py:448
  114.8 1.4 %out.1 = (bf16[2,1,2,384,384]{4,3,2,1,0:T(8,128)(2,1)}, bf16[2,1,2,384,384]{4,3,2,1,0:T(8,128)(2,1)}) custom-call(bf16[2,3,2,2,128,384]{5,4,3,2,1,0:T(8,128)(2,1)S(1)} %gw.1.ob), custom_call_target="tpu_custom_call" | custom-call | tf_op jit(solution)/shard_map/out/pallas_call | solution.py:480

commit v5 on v4

--- a/solution.py
+++ b/solution.py
@@ -67,6 +67,9 @@
 STEPS = [((k // 8 + k // 2 % 4) % 4, k % 2, k // 2 % 4) for k in range(PIECES)]
 
 
+FIRST = (0, 1, 8, 3, 2, 24, 16, 4, 9, 11, 25, 5, 12)
+
+
 def mirror(t):
     return (t // 8) * 8 + (1 - lax.rem(t // 4, 2)) * 4 + lax.rem(t, 4)
 
@@ -78,7 +81,7 @@
 def kernel(
     lg, gg, cb, fwd_h, pol_h, sig_h, ob,
     gin, s0, xb, ps, pr, p3, lf, acc, sc, ss, sx, fs, fr, cc, rr, fwd, pol, sig,
-    in_sem, tab_sem, self_sem, send_sem, recv_sem, near_send, near_recv,
+    in_sem, tab_sem, self_sem, send_sem, recv_sem, near_send, near_recv, go_sem, met_sem,
 ):
     me = lax.axis_index("energy")
     b = lax.axis_index("blk")
@@ -109,7 +112,7 @@
         )
     pl.semaphore_signal(barrier, inc=1, device_id=core_id, device_id_type=MESH)
 
-    @pl.when(inner)
+    @pl.when(b == 1)
     def _():
         pl.semaphore_signal(barrier, inc=1, device_id=cross_id, device_id_type=MESH)
 
@@ -137,12 +140,28 @@
             )
 
     def exchange(stage, part, source, dest, span):
-        for t, lag in peers[1:]:
+        def one(t, lag):
             pltpu.make_async_remote_copy(
                 src_ref=source(t, lag), dst_ref=dest(), send_sem=send_sem.at[stage, part],
                 recv_sem=recv_sem.at[stage, part], device_id={"energy": t, "blk": b},
                 device_id_type=MESH,
             ).start()
+
+        if stage == 3:
+            for t in FIRST:
+
+                @pl.when(me != t)
+                def _():
+                    one(t, t)
+
+            for t, lag in peers[1:]:
+
+                @pl.when(functools.reduce(jnp.logical_and, [t != f for f in FIRST]))
+                def _():
+                    one(t, lag)
+        else:
+            for t, lag in peers[1:]:
+                one(t, lag)
         pltpu.make_async_copy(source(me, my_lag), dest(), self_sem.at[stage, part]).start()
 
     def arrived(stage, part, source, dest, span):
@@ -195,7 +214,18 @@
 
         lax.fori_loop(0, 6, pack, 0)
         if c == 0:
-            pl.semaphore_wait(barrier, jnp.where(inner, PIECES + 1, PIECES))
+            pl.semaphore_wait(barrier, jnp.where(b == 2, PIECES + 1, PIECES))
+
+            @pl.when(b == 2)
+            def _():
+                pl.semaphore_signal(met_sem, inc=1, device_id=cross_id, device_id_type=MESH)
+
+        if c == 1:
+
+            @pl.when(b == 3)
+            def _():
+                pl.semaphore_wait(go_sem, 1)
+
         exchange(*st0(c))
 
     for copy in tables:
@@ -217,6 +247,10 @@
 
     def polarize(c, carry):
         arrived(*st0(c))
+
+        @pl.when(jnp.logical_and(c == 0, b == 2))
+        def _():
+            pl.semaphore_signal(go_sem, inc=1, device_id=core_id, device_id_type=MESH)
 
         def one(r, carry):
             cross = []
@@ -237,8 +271,6 @@
         return carry
 
     lax.fori_loop(0, 3, polarize, 0)
-
-    exchange(*st1(1, 0))
 
     def near_copy(k, c, slot):
         return pltpu.make_async_remote_copy(
@@ -334,14 +366,19 @@
                 )
         exchange(*st2(k, r))
 
+    @pl.when(b == 1)
+    def _():
+        pl.semaphore_wait(met_sem, 1)
+
     unpack(0, 0)
+    exchange(*st1(1, 0))
+    unpack(0, 1)
     exchange(*st1(1, 1))
-    unpack(0, 1)
-    exchange(*st1(1, 2))
     left(0, 0, 0)
     left(0, 0, 1)
     beside(0, 0)
     unpack(0, 2)
+    exchange(*st1(1, 2))
     left(0, 0, 2)
     beside(0, 1)
     beside(0, 2)
@@ -470,7 +507,7 @@
             pltpu.VMEM((8 * NE, 4 * LENGTH), BF),
             pltpu.VMEM((4 * NE, 4 * LENGTH), BF),
             dma((3, 2)), dma((9,)), dma((4, 6)), dma((4, 6)), dma((4, 6)), dma((2, 3, 3)),
-            dma((2, 3, 3)),
+            dma((2, 3, 3)), pltpu.SemaphoreType.REGULAR, pltpu.SemaphoreType.REGULAR,
         ],
         compiler_params=pltpu.CompilerParams(
             collective_id=0, has_side_effects=True, vmem_limit_bytes=60_000_000

time: 117 us -> 115 us (0.983)
  Pallas kernels: 116 us -> 114 us
    pallas_call x1, Pallas kernels: 114 us -> 112 us  [local(): pl.pallas_call(kernel, out_shape=pltpu.VMEM((2, 3, 2, 2, 128, ROWS), BF),...]
where the time goes in v5:
time: 115 us
  Pallas kernels  114 us (99%)
    pallas_call x1, Pallas kernels, local(): pl.pallas_call(kernel, out_shape=pltpu.VMEM((2, 3, 2, 2, 128, ROWS), BF),...  112 us

profile of v5, /device:TPU:1, one launch (start us, length us, event | category | flops | bytes accessed | tf_op | source)
XLA Modules:
  0.0 114.7 jit_solution(17090022240753403307)
XLA Ops:
  0.6 112.4 %gw.1.ob = bf16[2,3,2,2,128,384]{5,4,3,2,1,0:T(8,128)(2,1)S(1)} custom-call(bf16[2,1,2,384,384]{4,3,2,1,0:T(8,128)(2,1)} %lg.1, bf16[2,1,2,384,384]{4,3,2,1,0:T(8,128)(2,1)} %gg.1, bf16[1,3,2,384,384]{4,3,2,1,0:T(8,128)(2,1)} %cb.1, bf16[512,256]{1,0:T(8,128)(2,1)} %constant.12.fwd_h, bf16[512,512]{1,0:T(8,128)(2,1)} %constant.13.pol_h, ...), custom_call_target="tpu_custom_call" | custom-call | tf_op jit(solution)/shard_map/gw/pallas_call | solution.py:485
  113.1 1.4 %out.1 = (bf16[2,1,2,384,384]{4,3,2,1,0:T(8,128)(2,1)}, bf16[2,1,2,384,384]{4,3,2,1,0:T(8,128)(2,1)}) custom-call(bf16[2,3,2,2,128,384]{5,4,3,2,1,0:T(8,128)(2,1)S(1)} %gw.1.ob), custom_call_target="tpu_custom_call" | custom-call | tf_op jit(solution)/shard_map/out/pallas_call | solution.py:517

commit v6 on v5

--- a/solution.py
+++ b/solution.py
@@ -440,35 +440,32 @@
             for k in range(2):
                 near_copy(k, r, 2).wait_send()
 
-    for k in range(2):
-
-        def finish(r, carry):
-            arrived(*st3(k, r))
-            for c in range(3):
-                for j in range(2):
-                    x = fr[k, r, 16 * j : 16 * j + 16, :, c].reshape(32, 8, LANES)
-                    x = jnp.swapaxes(x, 0, 1)
-                    for h in range(2):
-                        at = 64 * h + 32 * j
-                        ob[k, r, :, :, at : at + 32, LANES * c : LANES * c + LANES] = x[
-                            4 * h : 4 * h + 4
-                        ].reshape(2, 2, 32, LANES)
-            return carry
-
-        lax.fori_loop(0, 3, finish, 0)
-
+    def finish(k, r):
+        arrived(*st3(k, r))
+        for c in range(3):
+            for j in range(2):
+                x = fr[k, r, 16 * j : 16 * j + 16, :, c].reshape(32, 8, LANES)
+                x = jnp.swapaxes(x, 0, 1)
+                for h in range(2):
+                    at = pl.multiple_of(128 * r + 64 * h + 32 * j, 32)
+                    ob[k, :, :, pl.ds(at, 32), LANES * c : LANES * c + LANES] = x[
+                        4 * h : 4 * h + 4
+                    ].reshape(2, 2, 32, LANES)
+
+    def most(m, carry):
+        finish(m // 3, lax.rem(m, 3))
+        return carry
+
+    lax.fori_loop(0, 5, most, 0)
     for k in range(2):
         for r in range(3):
             sent(*[st3(k, r)[i] for i in (0, 1, 4)])
+    finish(1, 2)
 
 
 def write_out(ob, ol, og, sem):
     copies = [
-        pltpu.make_async_copy(
-            ob.at[k, r], (ol, og)[k].at[:, 0, :, pl.ds(128 * r, 128), :], sem.at[k, r]
-        )
-        for k in range(2)
-        for r in range(3)
+        pltpu.make_async_copy(ob.at[k], (ol, og)[k].at[:, 0], sem.at[k]) for k in range(2)
     ]
     for copy in copies:
         copy.start()
@@ -484,7 +481,7 @@
     dma = pltpu.SemaphoreType.DMA
     held = pl.pallas_call(
         kernel,
-        out_shape=pltpu.VMEM((2, 3, 2, 2, 128, ROWS), BF),
+        out_shape=pltpu.VMEM((2, 2, 2, ROWS, ROWS), BF),
         in_specs=[any_spec] * 6,
         out_specs=pl.BlockSpec(memory_space=pltpu.VMEM),
         scratch_shapes=[
@@ -519,7 +516,7 @@
         out_shape=(out, out),
         in_specs=[any_spec],
         out_specs=(any_spec, any_spec),
-        scratch_shapes=[dma((2, 3))],
+        scratch_shapes=[dma((2,))],
         compiler_params=pltpu.CompilerParams(vmem_limit_bytes=1_000_000),
         name="out",
     )(held)

time: 115 us -> 115 us (level)
  no operation moved by 1% of the time
where the time goes in v6:
time: 115 us
  Pallas kernels  114 us (99%)
    pallas_call x1, Pallas kernels, local(): pl.pallas_call(kernel, out_shape=pltpu.VMEM((2, 2, 2, ROWS, ROWS), BF), i...  112 us

profile of v6, /device:TPU:1, one launch (start us, length us, event | category | flops | bytes accessed | tf_op | source)
XLA Modules:
  0.0 114.6 jit_solution(3797623395890061272)
XLA Ops:
  0.6 112.4 %gw.1.ob = bf16[2,2,2,384,384]{4,3,2,1,0:T(8,128)(2,1)S(1)} custom-call(bf16[2,1,2,384,384]{4,3,2,1,0:T(8,128)(2,1)} %lg.1, bf16[2,1,2,384,384]{4,3,2,1,0:T(8,128)(2,1)} %gg.1, bf16[1,3,2,384,384]{4,3,2,1,0:T(8,128)(2,1)} %cb.1, bf16[512,256]{1,0:T(8,128)(2,1)} %constant.12.fwd_h, bf16[512,512]{1,0:T(8,128)(2,1)} %constant.13.pol_h, ...), custom_call_target="tpu_custom_call" | custom-call | tf_op jit(solution)/shard_map/gw/pallas_call | solution.py:482
  113.0 1.4 %out.1 = (bf16[2,1,2,384,384]{4,3,2,1,0:T(8,128)(2,1)}, bf16[2,1,2,384,384]{4,3,2,1,0:T(8,128)(2,1)}) custom-call(bf16[2,2,2,384,384]{4,3,2,1,0:T(8,128)(2,1)S(1)} %gw.1.ob), custom_call_target="tpu_custom_call" | custom-call | tf_op jit(solution)/shard_map/out/pallas_call | solution.py:514

commit v7 on v6

--- a/solution.py
+++ b/solution.py
@@ -81,7 +81,7 @@
 def kernel(
     lg, gg, cb, fwd_h, pol_h, sig_h, ob,
     gin, s0, xb, ps, pr, p3, lf, acc, sc, ss, sx, fs, fr, cc, rr, fwd, pol, sig,
-    in_sem, tab_sem, self_sem, send_sem, recv_sem, near_send, near_recv, go_sem, met_sem,
+    in_sem, tab_sem, self_sem, send_sem, recv_sem, near_send, near_recv, go_sem, met_sem, turn_sem,
 ):
     me = lax.axis_index("energy")
     b = lax.axis_index("blk")
@@ -405,7 +405,17 @@
 
     def convolve(m, carry):
         k, r = m // 3, lax.rem(m, 3)
+
+        @pl.when(jnp.logical_and(m == 3, jnp.logical_not(inner)))
+        def _():
+            pl.semaphore_wait(turn_sem, 1)
+
         arrived(*st2(k, r))
+
+        @pl.when(jnp.logical_and(m == 3, inner))
+        def _():
+            pl.semaphore_signal(turn_sem, inc=1, device_id=core_id, device_id_type=MESH)
+
         half = fwd[pl.ds(pl.multiple_of(256 * k, 256), 256), :]
 
         def one(c, carry):
@@ -505,6 +515,7 @@
             pltpu.VMEM((4 * NE, 4 * LENGTH), BF),
             dma((3, 2)), dma((9,)), dma((4, 6)), dma((4, 6)), dma((4, 6)), dma((2, 3, 3)),
             dma((2, 3, 3)), pltpu.SemaphoreType.REGULAR, pltpu.SemaphoreType.REGULAR,
+            pltpu.SemaphoreType.REGULAR,
         ],
         compiler_params=pltpu.CompilerParams(
             collective_id=0, has_side_effects=True, vmem_limit_bytes=60_000_000

time: 115 us -> 115 us (level)
  no operation moved by 1% of the time
where the time goes in v7:
time: 115 us
  Pallas kernels  114 us (99%)
    pallas_call x1, Pallas kernels, local(): pl.pallas_call(kernel, out_shape=pltpu.VMEM((2, 2, 2, ROWS, ROWS), BF), i...  112 us

profile of v7, /device:TPU:1, one launch (start us, length us, event | category | flops | bytes accessed | tf_op | source)
XLA Modules:
  0.0 114.6 jit_solution(11387134078130363594)
XLA Ops:
  0.6 112.4 %gw.1.ob = bf16[2,2,2,384,384]{4,3,2,1,0:T(8,128)(2,1)S(1)} custom-call(bf16[2,1,2,384,384]{4,3,2,1,0:T(8,128)(2,1)} %lg.1, bf16[2,1,2,384,384]{4,3,2,1,0:T(8,128)(2,1)} %gg.1, bf16[1,3,2,384,384]{4,3,2,1,0:T(8,128)(2,1)} %cb.1, bf16[512,256]{1,0:T(8,128)(2,1)} %constant.12.fwd_h, bf16[512,512]{1,0:T(8,128)(2,1)} %constant.13.pol_h, ...), custom_call_target="tpu_custom_call" | custom-call | tf_op jit(solution)/shard_map/gw/pallas_call | solution.py:492
  113.1 1.4 %out.1 = (bf16[2,1,2,384,384]{4,3,2,1,0:T(8,128)(2,1)}, bf16[2,1,2,384,384]{4,3,2,1,0:T(8,128)(2,1)}) custom-call(bf16[2,2,2,384,384]{4,3,2,1,0:T(8,128)(2,1)S(1)} %gw.1.ob), custom_call_target="tpu_custom_call" | custom-call | tf_op jit(solution)/shard_map/out/pallas_call | solution.py:525
